TPU v7x, 512 devices: a whole 4x4x16 slice. The times are simulated.
512 devices in a mesh: tile: 64 (over x, z_lo, core), agent: 8 (over z_hi, y).
Axes of the slice: x: 4, y: 4, z: 16 (z_hi: 2, z_lo: 8; z = z_hi * 8 + z_lo), core: 2. Of those that a mesh axis runs over, the one named last changes fastest.
Arguments:
- states: float32 [8, 8, 128, 256], P('agent', None, 'tile'), may hold values from -6 to 6
- footprints: float32 [64, 64, 64, 512], P('agent', 'tile'), may hold values from -0.25 to 0.25
- offsets: int32 [64, 64], P('agent', 'tile'), may hold values from 0 to 1984, as said below
- measured: float32 [64, 8, 2048], P('agent', None, 'tile'), may hold values from -9 to 9
- weights: float32 [64, 8, 2048], P('agent', None, 'tile'), may hold values from 0.2 to 5
Outputs:
- new_states: float32 [8, 8, 128, 256], P('agent', None, 'tile')
- prior_volume: float32 [8, 128, 256], P(None, 'tile')
Inputs may be any that keep to these rules, and one draw needn't show every extreme that they name: For one agent and one tile t, the values offsets[v, t] // 32 differ between the agent's 8 views v.
All inputs are finite; a program needn't handle non-finite values.
Results may differ from a plain program's by a relative error of at most 0.0003.
Values sent between devices are 32-bit elements; how exact they have to be, the bound alone decides.
No kernel may reach another device: no remote copies, remote signals or barrier semaphores. Data moves between devices by JAX's collectives and lax.ppermute only.
A program may use at most 64 MiB of HBM per device.

v0:
```python
import jax
import jax.numpy as jnp
from jax import lax
from jax.sharding import PartitionSpec as P

SWEEPS = 2


STEP_SIZE = 0.25
RELAX = 0.6
QRATIO = 0.6


def with_halo(value, sides, width):
    for axis, dim in sides:
        count, length = (lax.axis_size(axis), value.shape[dim])
        up = [(i, (i + 1) % count) for i in range(count - 1)]
        down = [(j, i) for i, j in up]
        last = lax.slice_in_dim(value, length - width, length, axis=dim)
        first = lax.slice_in_dim(value, 0, width, axis=dim)
        before = lax.ppermute(last, axis, up)
        after = lax.ppermute(first, axis, down)
        value = jnp.concatenate([before, value, after], axis=dim)
    return value


def neighbour_table():
    offsets_nb = []
    for a in (-1, 0, 1):
        for b in (-1, 0, 1):
            for c in (-1, 0, 1):
                if a != 0 or b != 0 or c != 0:
                    offsets_nb.append((a, b, c, 1.0 / (a * a + b * b + c * c) ** 0.5))
    total = sum((item[3] for item in offsets_nb))
    return [(a, b, c, 4.0 * w / total) for a, b, c, w in offsets_nb]


def sweep_update(padded, average):
    depth, height, width = average.shape
    centre = padded[1 : 1 + depth, 1 : 1 + height, 1 : 1 + width]
    numerator = average
    denominator = jnp.ones_like(average)
    for a, b, c, weight_nb in neighbour_table():
        neighbour = padded[1 + a : 1 + a + depth, 1 + b : 1 + b + height, 1 + c : 1 + c + width]
        differ = centre - neighbour
        powered = jnp.power(differ * differ, 0.4)
        coefficient = weight_nb * (1.0 + QRATIO * powered) / ((1.0 + powered) * (1.0 + powered))
        numerator = numerator + coefficient * neighbour
        denominator = denominator + coefficient
    return numerator / denominator


def shards(states, footprints, offsets, measured, weights):
    current = states[0]
    blocks = footprints[:, 0]
    offsets_dev = offsets[:, 0]
    slices, height, width = current.shape
    views, foot, pixels = blocks.shape
    share = measured.shape[2]
    n_tile = lax.axis_size("tile")
    detector = share * n_tile
    n_agent = lax.axis_size("agent")
    zero_index = jnp.int32(0)
    volume = current.reshape(slices, pixels)
    projected = jnp.einsum("sp,vbp->vsb", volume, blocks, precision=lax.Precision.HIGHEST)
    partial_value = jnp.stack(
        [
            lax.dynamic_update_slice(
                jnp.zeros((slices, detector), jnp.float32),
                projected[view],
                (zero_index, offsets_dev[view]),
            )
            for view in range(views)
        ]
    )
    share_sum = lax.psum_scatter(partial_value, "tile", scatter_dimension=2, tiled=True)
    residual_share = weights * (share_sum - measured)
    residual = lax.all_gather(residual_share, "tile", axis=2, tiled=True)
    windows = jnp.stack(
        [
            lax.dynamic_slice(residual[view], (zero_index, offsets_dev[view]), (slices, foot))
            for view in range(views)
        ]
    )
    gradient = jnp.einsum("vsb,vbp->sp", windows, blocks, precision=lax.Precision.HIGHEST)
    fitted = current - STEP_SIZE * gradient.reshape(slices, height, width)
    reflect = 2.0 * fitted - current
    brick_mean = lax.psum_scatter(reflect, "agent", scatter_dimension=0, tiled=True) / n_agent
    smoothed = brick_mean
    for sweep_index in range(SWEEPS):
        padded = with_halo(smoothed, (("tile", 1), ("agent", 0)), 1)
        padded = jnp.pad(padded, ((0, 0), (0, 0), (1, 1)))
        smoothed = sweep_update(padded, brick_mean)
    prior_vol = lax.all_gather(smoothed, "agent", axis=0, tiled=True)
    current = (1.0 - RELAX) * current + RELAX * (2.0 * prior_vol - reflect)
    return (current[None], prior_vol)


def solution(mesh):
    in_specs = (
        P("agent", None, "tile", None),
        P("agent", "tile", None, None),
        P("agent", "tile"),
        P("agent", None, "tile"),
        P("agent", None, "tile"),
    )
    out_specs = (P("agent", None, "tile", None), P(None, "tile", None))
    return jax.shard_map(shards, mesh=mesh, in_specs=in_specs, out_specs=out_specs, check_vma=False)
```

profile of v0, /device:TPU:24, one launch (start us, length us, event | category | flops | bytes accessed | tf_op | source)
XLA Modules:
  0.0 878.2 jit_solution(8798802146423708650)
XLA Ops:
  7.2 1.6 fusion.17
  19.1 0.7 reshape.62
  19.8 2.6 convolution_bitcast_fusion
  23.0 0.3 dynamic_update_slice.32
  24.0 0.3 dynamic_update_slice.33
  24.9 0.3 dynamic_update_slice.34
  25.9 0.3 dynamic_update_slice.35
  27.0 0.3 dynamic_update_slice.36
  28.0 0.3 dynamic_update_slice.37
  28.9 0.3 dynamic_update_slice.38
  29.9 0.3 dynamic_update_slice.39
  30.3 4.6 copy.26
  34.9 6.5 reshape.66
  41.3 1.3 dynamic-slice.8
  42.6 444.3 %reduce-scatter.4.cloned.1.call-done = f32[32,64]{1,0:T(8,128)} async-done(((f32[2048,64]{1,0:T(8,128)}), f32[32,64]{1,0:T(8,128)}) %reduce-scatter.4.cloned.1.call-update) | async-done | bytes 8208
  487.0 0.8 reshape.67
  487.8 0.1 copy.27
  487.9 0.1 copy.12
  488.0 166.6 %all_gather.6 = f32[8,8,2048]{1,0,2:T(8,128)} all-gather(f32[8,8,32]{1,0,2:T(8,128)S(1)} %copy.12), channel_id=1, replica_groups=mesh['tile'=64,'agent'=8] {'tile'}, dimensions={2}, use_global_device_ids=true | all-gather | bytes 532480 | tf_op jit(solution)/shard_map/all_gather | solution.py:78
  654.6 29.4 %fusion.13 = (f32[1,8,2048]{1,0,2:T(1,128)}, f32[1,8,2048]{1,0,2:T(1,128)}, f32[1,8,2048]{1,0,2:T(1,128)}, f32[1,8,2048]{1,0,2:T(1,128)}, f32[1,8,2048]{1,0,2:T(...) fusion(f32[8,8,2048]{1,0,2:T(8,128)} %all_gather.6), kind=kLoop, calls=%fused_computation.61 | loop fusion | bytes 1048576 | tf_op jit(solution)/shard_map/slice | solution.py:81
  684.0 0.8 constant_dynamic-slice_fusion
  684.8 0.1 copy.41
  684.9 0.8 constant_dynamic-slice_fusion.2
  685.7 0.1 copy.37
  685.7 0.8 constant_dynamic-slice_fusion.4
  686.6 0.1 copy.29
  687.0 0.6 fusion.3
  687.6 65.1 %all-reduce.2 = f32[8,2,256]{2,1,0:T(2,128)S(1)} all-reduce(f32[8,2,256]{2,1,0:T(2,128)S(1)} %copy.22), channel_id=3, replica_groups=mesh['tile'=64,'agent'=8] {'agent'}, use_global_device_ids=true, to_apply=%region_1.0.clone | all-reduce | flops 4096 | bytes 32768
  752.7 0.7 dynamic-slice_multiply_fusion
  753.4 1.3 collective-permute-start
  754.7 1.3 collective-permute-start.1
  756.0 1.7 collective-permute-done.1
  757.8 15.0 %collective-permute-start.2 = (f32[1,4,256]{2,1,0:T(4,128)S(1)}, f32[1,4,256]{2,1,0:T(4,128)S(1)}, u32[]{:S(2)}, u32[]{:S(2)}) collective-permute-start(f32[1,4,256]{2,1,0:T(4,128)S(1)} %pad_maximum_fusion), channel_id=1, source_target_pairs={{0,1},{1,2},{2,3},{3,4},{4,5},{5,6},{6,7},{8,9},{9,10},{10,11},{11... | collective-permute-start | bytes 12296 | tf_op jit(solution)/shard_map/ppermute | solution.py:21
  772.8 1.9 collective-permute-start.3
  774.7 14.4 %collective-permute-done.3 = f32[1,4,256]{2,1,0:T(4,128)S(1)} collective-permute-done((f32[1,4,256]{2,1,0:T(4,128)S(1)}, f32[1,4,256]{2,1,0:T(4,128)S(1)}, u32[]{:S(2)}, u32[]{:S(2)}) %collective-permute-start.3) | collective-permute-done | bytes 4128 | tf_op jit(solution)/shard_map/ppermute | solution.py:22
  789.1 0.1 select_maximum_fusion.4
  789.2 0.2 add_divide_fusion.1
  789.4 1.3 collective-permute-start.4
  790.7 1.3 collective-permute-start.5
  792.1 1.7 collective-permute-done.5
  793.8 1.9 collective-permute-start.6
  795.7 3.9 collective-permute-start.7
  799.7 12.4 %collective-permute-done.7 = f32[1,4,256]{2,1,0:T(4,128)S(1)} collective-permute-done((f32[1,4,256]{2,1,0:T(4,128)S(1)}, f32[1,4,256]{2,1,0:T(4,128)S(1)}, u32[]{:S(2)}, u32[]{:S(2)}) %collective-permute-start.7) | collective-permute-done | bytes 4128 | tf_op jit(solution)/shard_map/ppermute | solution.py:22
  812.1 0.1 select_maximum_fusion
  812.2 0.9 add_divide_fusion
  813.0 57.1 %all_gather.7 = f32[8,2,256]{2,1,0:T(2,128)S(1)} all-gather(f32[1,2,256]{2,1,0:T(2,128)S(1)} %add_divide_fusion), channel_id=1, replica_groups=mesh['tile'=64,'agent'=8] {'agent'}, dimensions={0}, use_global_device_ids=true | all-gather | bytes 18432 | tf_op jit(solution)/shard_map/all_gather | solution.py:94
  870.2 0.6 copy.24
  870.8 0.6 copy.81
  (52 shorter events, 0.6 us)
Async XLA Ops:
  7.2 479.8 %reduce-scatter.4.cloned.1.call-start = ((), (), s32[]{:S(2)}) async-start(), calls=%async_computation.1 | async-start | bytes 1064960
  30.2 457.6 %copy-start.2 = (f32[8,8,32]{2,1,0:T(8,128)S(1)}, f32[8,8,32]{2,1,0:T(8,128)}, u32[]{:S(2)}) copy-start(f32[8,8,32]{2,1,0:T(8,128)} %param.9) | copy-start | bytes 24580
  30.2 457.6 %copy-start.3 = (f32[8,8,32]{2,1,0:T(8,128)S(1)}, f32[8,8,32]{2,1,0:T(8,128)}, u32[]{:S(2)}) copy-start(f32[8,8,32]{2,1,0:T(8,128)} %param.8) | copy-start | bytes 24580
  654.6 32.4 %copy-start = (f32[8,1,64,512]{3,2,1,0:T(8,128)S(1)}, f32[8,1,64,512]{3,2,1,0:T(8,128)}, u32[]{:S(2)}) copy-start(f32[8,1,64,512]{3,2,1,0:T(8,128)} %param.6) | copy-start | bytes 3145732
  654.6 32.4 %copy-start.1 = (f32[1,8,2,256]{3,2,1,0:T(2,128)S(1)}, f32[1,8,2,256]{3,2,1,0:T(2,128)}, u32[]{:S(2)}) copy-start(f32[1,8,2,256]{3,2,1,0:T(2,128)} %param.5) | copy-start | bytes 49156
  753.4 2.6 collective-permute-start
  754.7 3.1 collective-permute-start.1
  757.8 16.9 %collective-permute-start.2 = (f32[1,4,256]{2,1,0:T(4,128)S(1)}, f32[1,4,256]{2,1,0:T(4,128)S(1)}, u32[]{:S(2)}, u32[]{:S(2)}) collective-permute-start(f32[1,4,256]{2,1,0:T(4,128)S(1)} %pad_maximum_fusion), channel_id=1, source_target_pairs={{0,1},{1,2},{2,3},{3,4},{4,5},{5,6},{6,7},{8,9},{9,10},{10,11},{11... | collective-permute-start | bytes 12296 | tf_op jit(solution)/shard_map/ppermute | solution.py:21
  772.8 16.3 %collective-permute-start.3 = (f32[1,4,256]{2,1,0:T(4,128)S(1)}, f32[1,4,256]{2,1,0:T(4,128)S(1)}, u32[]{:S(2)}, u32[]{:S(2)}) collective-permute-start(f32[1,4,256]{2,1,0:T(4,128)S(1)} %pad_maximum_fusion), channel_id=1, source_target_pairs={{1,0},{2,1},{3,2},{4,3},{5,4},{6,5},{7,6},{9,8},{10,9},{11,10},{12... | collective-permute-start | bytes 12296 | tf_op jit(solution)/shard_map/ppermute | solution.py:22
  789.4 2.6 collective-permute-start.4
  790.7 3.1 collective-permute-start.5
  793.8 5.9 collective-permute-start.6
  795.7 16.3 %collective-permute-start.7 = (f32[1,4,256]{2,1,0:T(4,128)S(1)}, f32[1,4,256]{2,1,0:T(4,128)S(1)}, u32[]{:S(2)}, u32[]{:S(2)}) collective-permute-start(f32[1,4,256]{2,1,0:T(4,128)S(1)} %pad_maximum_fusion.1), channel_id=1, source_target_pairs={{1,0},{2,1},{3,2},{4,3},{5,4},{6,5},{7,6},{9,8},{10,9},{11,10},{12... | collective-permute-start | bytes 12296 | tf_op jit(solution)/shard_map/ppermute | solution.py:22
Sparse Core Ops, SparseCore 0:
  41.5 445.4 reduce-scatter.3
where the time goes:
time: 879 us; the launch traced here: 878 us
  waiting for transfers between devices  475 us (54%)
  blocking collectives  289 us (33%)
  local copies, waits for them, and re-layouts  51.8 us (6%)
  between operations  29.8 us (3%)
  starting transfers between devices  28 us (3%)
    unnamed x2, waiting for transfers between devices  444 us
    all_gather x1, blocking collectives, shards(): residual = lax.all_gather(residual_share, 'tile', axis=2, tiled=True)  167 us
    unnamed x1, blocking collectives  65.1 us
    all_gather x1, blocking collectives, shards(): prior_vol = lax.all_gather(smoothed, 'agent', axis=0, tiled=True)  57.1 us
    ppermute x4, waiting for transfers between devices, with_halo(): after = lax.ppermute(first, axis, down)  30.3 us
    slice x1, local copies, waits for them, and re-layouts, shards(): residual[view]  29.4 us
    ppermute x4, starting transfers between devices, with_halo(): before = lax.ppermute(last, axis, up)  19.5 us
  transfers between devices with their start and end apart: 9, of which 5 were waited for; matrix products, arithmetic and copies ran while one was open for 0% of the time, Pallas kernels for 0%

commit v1 on v0

v1 whole, which is shorter than its diff:
```python
import jax
import jax.numpy as jnp
from jax import lax
from jax.experimental import pallas as pl
from jax.experimental.pallas import tpu as pltpu
from jax.sharding import PartitionSpec as P

SWEEPS = 2
STEP_SIZE = 0.25
RELAX = 0.6
QRATIO = 0.6
BLOCK = 32
LANES = 128

SMEM = pl.BlockSpec(memory_space=pltpu.SMEM)
VMEM = pl.BlockSpec(memory_space=pltpu.VMEM)


def neighbour_table():
    offsets_nb = []
    for a in (-1, 0, 1):
        for b in (-1, 0, 1):
            for c in (-1, 0, 1):
                if a != 0 or b != 0 or c != 0:
                    offsets_nb.append((a, b, c, 1.0 / (a * a + b * b + c * c) ** 0.5))
    total = sum((item[3] for item in offsets_nb))
    return [(a, b, c, 4.0 * w / total) for a, b, c, w in offsets_nb]


def halves(x):
    high = x.astype(jnp.bfloat16)
    return high, (x - high.astype(jnp.float32)).astype(jnp.bfloat16)


def split_dot(small, large, dims):
    rows = small.shape[0]
    stacked = jnp.concatenate([x.astype(jnp.float32) for x in halves(small)], axis=0).astype(jnp.bfloat16)
    total = None
    for part in halves(large):
        both = lax.dot_general(stacked, part, (dims, ((), ())), preferred_element_type=jnp.float32)
        both = both[:rows] + both[rows:]
        total = both if total is None else total + both
    return total


def lane_iota(shape):
    return lax.broadcasted_iota(jnp.int32, shape, len(shape) - 1)


def project_kernel(offsets_ref, states_ref, blocks_ref, measured_ref, weights_ref, out_ref):
    views, _, foot, pixels = blocks_ref.shape
    slices, width = states_ref.shape[1], states_ref.shape[3]
    share = measured_ref.shape[2]
    lane = lane_iota((slices, LANES))
    blocks = blocks_ref[:, 0].reshape(views * foot, pixels)
    projected = split_dot(states_ref[0, :, 0, :], blocks[:, :width], ((1,), (1,)))
    projected += split_dot(states_ref[0, :, 1, :], blocks[:, width:], ((1,), (1,)))
    step = pl.program_id(0)
    per_vreg = LANES // foot
    blank = jnp.zeros((slices, LANES - share), jnp.float32)
    for local in range(views):
        view = step * views + local
        offset = offsets_ref[view, 0]
        base = offset // BLOCK
        shift = offset - base * BLOCK
        at = (local % per_vreg) * foot
        pair = projected[:, (local // per_vreg) * LANES : (local // per_vreg + 1) * LANES]
        band = jnp.where((lane >= at) & (lane < at + foot), pair, 0.0)
        band = pltpu.roll(band, (shift + LANES - at) % LANES, 1)
        first = band + jnp.concatenate([blank, measured_ref[local]], axis=1)
        second = jnp.concatenate([weights_ref[local], blank], axis=1)
        second = jnp.where(lane == share, base.astype(jnp.float32), second)
        start = view * 2 * slices
        out_ref[pl.ds(start, slices, stride=2), :] = first
        out_ref[pl.ds(start + 1, slices, stride=2), :] = second


def residual_kernel(in_ref, out_ref):
    tiles = out_ref.shape[0]
    share = BLOCK
    lane = lane_iota((tiles, LANES))
    first = in_ref[pl.ds(0, tiles, stride=2), :]
    second = in_ref[pl.ds(1, tiles, stride=2), :]
    base = second[:, share : share + 1].astype(jnp.int32)
    onehot = jnp.where(lane_iota((tiles, tiles)) == base, 1.0, 0.0)
    placed = lax.dot_general(
        onehot, first, (((0,), (0,)), ((), ())), precision=lax.Precision.HIGHEST, preferred_element_type=jnp.float32
    )
    total = placed
    for part in (1, 2):
        moved = pltpu.roll(placed, part, 0)
        total += pltpu.roll(moved, LANES - part * share, 1)
    measured = pltpu.roll(first, share, 1)
    residual = jnp.where(lane < share, second * (total - measured), 0.0)
    windows = residual
    for part in (1, 2):
        moved = pltpu.roll(residual, tiles - part, 0)
        windows += pltpu.roll(moved, part * share, 1)
    out_ref[...] = jnp.dot(onehot, windows, precision=lax.Precision.HIGHEST, preferred_element_type=jnp.float32)


def gradient_kernel(offsets_ref, windows_ref, states_ref, blocks_ref, out_ref):
    views, _, foot, pixels = blocks_ref.shape
    slices, width = states_ref.shape[1], states_ref.shape[3]
    copies = out_ref.shape[0]
    lane = lane_iota((slices, LANES))
    per_vreg = LANES // foot
    pieces = []
    for view in range(views):
        offset = offsets_ref[view, 0]
        shift = offset - (offset // BLOCK) * BLOCK
        at = (view % per_vreg) * foot
        window = windows_ref[view * slices : (view + 1) * slices, :]
        window = pltpu.roll(window, (LANES + at - shift) % LANES, 1)
        if at == 0:
            pieces.append(window)
        else:
            pieces[-1] = jnp.where(lane >= at, window, pieces[-1])
    windows = jnp.concatenate(pieces, axis=1)
    blocks = blocks_ref[:, 0].reshape(views * foot, pixels)
    gradient = split_dot(windows, blocks, ((1,), (0,)))
    for row in range(2):
        at = slice(row * width, (row + 1) * width)
        reflect = states_ref[0, :, row, :] - (2.0 * STEP_SIZE) * gradient[:, at]
        for copy in range(copies):
            out_ref[copy, :, at] = reflect


def mean_kernel(in_ref, out_ref):
    count = in_ref.shape[0]
    total = in_ref[0]
    for agent in range(1, count):
        total = total + in_ref[agent]
    out_ref[...] = total * (1.0 / count)


def shifted(row, a, c):
    slices, width = row.shape
    if a:
        where = lax.broadcasted_iota(jnp.int32, row.shape, 0)
        row = pltpu.roll(row, (slices - a) % slices, 0)
        row = jnp.where(where == (slices - 1 if a > 0 else 0), 0.0, row)
    if c:
        where = lane_iota(row.shape)
        row = pltpu.roll(row, (width - c) % width, 1)
        row = jnp.where(where == (width - 1 if c > 0 else 0), 0.0, row)
    return row


def sweep_rows(rows, averages):
    table = neighbour_table()
    moved = [{(a, c): shifted(row, a, c) for a in (-1, 0, 1) for c in (-1, 0, 1)} for row in rows]
    out = []
    for index, average in enumerate(averages):
        centre = rows[index + 1]
        numerator = average
        denominator = jnp.ones_like(average)
        for a, b, c, weight_nb in table:
            neighbour = moved[index + 1 + b][(a, c)]
            differ = centre - neighbour
            powered = jnp.exp(0.4 * jnp.log(differ * differ))
            above = 1.0 + powered
            coefficient = (weight_nb + (weight_nb * QRATIO) * powered) / (above * above)
            numerator = numerator + coefficient * neighbour
            denominator = denominator + coefficient
        out.append(numerator / denominator)
    return out


def prior_kernel(where_ref, mean_ref, near_ref, side_ref, states_ref, reflect_ref, new_ref, prior_ref):
    width = states_ref.shape[3]
    tile = where_ref[0]
    last = where_ref[1]
    odd = tile % 2 == 1
    near = near_ref[...]
    side = side_ref[...]
    mean = mean_ref[...]
    above = jnp.where(odd, near, side)
    below = jnp.where(odd, side, near)
    above = jnp.where(tile == 0, 0.0, above)
    below = jnp.where(tile == last, 0.0, below)
    rows = [x[:, i * width : (i + 1) * width] for x in (above, mean, below) for i in range(2)]
    averages = rows
    swept = sweep_rows(rows, averages[1:5])
    swept[0] = jnp.where(tile == 0, 0.0, swept[0])
    swept[3] = jnp.where(tile == last, 0.0, swept[3])
    final = sweep_rows(swept, averages[2:4])
    for row in range(2):
        reflect = reflect_ref[0, :, row * width : (row + 1) * width]
        prior_ref[:, row, :] = final[row]
        new_ref[0, :, row, :] = (1.0 - RELAX) * states_ref[0, :, row, :] + RELAX * (2.0 * final[row] - reflect)


def halo_pairs(n_tile, n_agent, per_x):
    near, side = [], []
    for tile in range(n_tile):
        for agent in range(n_agent):
            near.append((tile * n_agent + agent, (tile ^ 1) * n_agent + agent))
    for tile in range(1, n_tile - 1, 2):
        other = tile + 1
        for agent in range(n_agent):
            crossing = tile // per_x != other // per_x
            partner = (agent + n_agent // 2) % n_agent if crossing else agent
            one, two = tile * n_agent + agent, other * n_agent + partner
            side += [(one, two), (two, one)]
    return near, side


def shards(states, footprints, offsets, measured, weights):
    n_tile = lax.axis_size("tile")
    n_agent = lax.axis_size("agent")
    _, slices, height, width = states.shape
    views, _, foot, pixels = footprints.shape
    share = measured.shape[2]
    f32 = jnp.float32

    half = views // 2
    sent = pl.pallas_call(
        project_kernel,
        grid=(2,),
        in_specs=[
            SMEM,
            pl.BlockSpec(states.shape, lambda i: (0, 0, 0, 0)),
            pl.BlockSpec((half, 1, foot, pixels), lambda i: (i, 0, 0, 0)),
            pl.BlockSpec((half, slices, share), lambda i: (i, 0, 0)),
            pl.BlockSpec((half, slices, share), lambda i: (i, 0, 0)),
        ],
        out_specs=pl.BlockSpec((2 * n_tile, LANES), lambda i: (0, 0)),
        out_shape=jax.ShapeDtypeStruct((2 * n_tile, LANES), f32),
        name="project",
    )(offsets, states, footprints, measured, weights)
    bands = lax.all_to_all(sent.reshape(n_tile, 2, LANES), "tile", 0, 0, tiled=True)
    back = pl.pallas_call(
        residual_kernel,
        in_specs=[VMEM],
        out_specs=VMEM,
        out_shape=jax.ShapeDtypeStruct((n_tile, LANES), f32),
        name="residual",
    )(bands.reshape(2 * n_tile, LANES))
    windows = lax.all_to_all(back.reshape(n_tile, 1, LANES), "tile", 0, 0, tiled=True)
    copies = pl.pallas_call(
        gradient_kernel,
        in_specs=[SMEM, VMEM, VMEM, VMEM],
        out_specs=VMEM,
        out_shape=jax.ShapeDtypeStruct((n_agent, slices, pixels), f32),
        name="gradient",
    )(offsets, windows.reshape(n_tile, LANES), states, footprints)
    reflects = lax.all_to_all(copies, "agent", 0, 0, tiled=True)
    mean = pl.pallas_call(
        mean_kernel,
        in_specs=[VMEM],
        out_specs=VMEM,
        out_shape=jax.ShapeDtypeStruct((slices, pixels), f32),
        name="mean",
    )(reflects)
    near_pairs, side_pairs = halo_pairs(n_tile, n_agent, 16)
    side = lax.ppermute(mean, ("tile", "agent"), side_pairs)
    near = lax.ppermute(mean, ("tile", "agent"), near_pairs)
    where = jnp.stack([lax.axis_index("tile"), jnp.int32(n_tile - 1)]).astype(jnp.int32)
    new_states, prior = pl.pallas_call(
        prior_kernel,
        grid=(1,),
        in_specs=[
            SMEM,
            pl.BlockSpec((slices, pixels), lambda i: (0, 0)),
            pl.BlockSpec((slices, pixels), lambda i: (0, 0)),
            pl.BlockSpec((slices, pixels), lambda i: (0, 0)),
            pl.BlockSpec(states.shape, lambda i: (0, 0, 0, 0)),
            pl.BlockSpec((1, slices, pixels), lambda i: (0, 0, 0)),
        ],
        out_specs=[
            pl.BlockSpec(states.shape, lambda i: (0, 0, 0, 0)),
            pl.BlockSpec((slices, height, width), lambda i: (0, 0, 0)),
        ],
        out_shape=[
            jax.ShapeDtypeStruct(states.shape, f32),
            jax.ShapeDtypeStruct((slices, height, width), f32),
        ],
        name="prior",
    )(where, mean, near, side, states, copies)
    return new_states, prior


def solution(mesh):
    in_specs = (
        P("agent", None, "tile", None),
        P("agent", "tile", None, None),
        P("agent", "tile"),
        P("agent", None, "tile"),
        P("agent", None, "tile"),
    )
    out_specs = (P("agent", None, "tile", None), P(None, "tile", None))
    return jax.shard_map(shards, mesh=mesh, in_specs=in_specs, out_specs=out_specs, check_vma=False)
```

time: 879 us -> 96.4 us (0.11)
  the two profiles are of different devices: /device:TPU:24 before, /device:TPU:1 now
where the time goes in v1:
time: 96.4 us; the launch traced here: 95.9 us
  blocking collectives  47.4 us (49%)
  starting transfers between devices  18.9 us (20%)
  waiting for transfers between devices  15.3 us (16%)
  Pallas kernels  10.4 us (11%)
  local copies, waits for them, and re-layouts  2.57 us (3%)
    all_to_all x1, blocking collectives, shards(): lax.all_to_all(sent.reshape(n_tile, 2, LANES), 'tile', 0, 0, tiled=True)  29.9 us
    all_to_all x1, blocking collectives, shards(): lax.all_to_all(back.reshape(n_tile, 1, LANES), 'tile', 0, 0, tiled=True)  17.5 us
    all_to_all x1, waiting for transfers between devices, shards(): reflects = lax.all_to_all(copies, 'agent', 0, 0, tiled=True)  14.2 us
    all_to_all x1, starting transfers between devices, shards(): reflects = lax.all_to_all(copies, 'agent', 0, 0, tiled=True)  9.94 us
    ppermute x1, starting transfers between devices, shards(): side = lax.ppermute(mean, ('tile', 'agent'), side_pairs)  4.97 us
    ppermute x1, starting transfers between devices, shards(): near = lax.ppermute(mean, ('tile', 'agent'), near_pairs)  4.04 us
    unnamed x7, local copies, waits for them, and re-layouts  2.57 us
    pallas_call x1, Pallas kernels, shards(): pl.pallas_call(project_kernel, grid=(2,), in_specs=[SMEM, pl.BlockSpec(st...  2.36 us
  transfers between devices with their start and end apart: 3, of which 2 were waited for; matrix products, arithmetic and copies ran while one was open for 1% of the time, Pallas kernels for 0%

profile of v1, /device:TPU:1, one launch (start us, length us, event | category | flops | bytes accessed | tf_op | source)
XLA Modules:
  0.0 95.9 jit_solution(5255067527031690056)
XLA Ops:
  0.6 1.3 %copy.11.offsets_ref = s32[8,1]{1,0:T(8,128)} copy(s32[8,1]{0,1:T(1,128)} %param.7) | data formatting | bytes 64 | tf_op args[2]
  2.0 2.4 %project.1 = f32[128,128]{1,0:T(8,128)} custom-call(s32[8,1]{1,0:T(8,128)} %copy.11.offsets_ref, f32[1,8,2,256]{3,2,1,0:T(2,128)} %states_ref.5, f32[8,1,64,512]{3,2,1,0:T(8,128)} %blocks_ref.3, f32[8,8,32]{2,1,0:T(8,128)} %measured_ref.1, f32[8,8,32]{2,1,0:T(8,128)} %weights_ref.1), custom_call_target="tpu_custom_call" | custom-call | tf_op jit(solution)/shard_map/project/pallas_call | solution.py:218
  4.3 29.9 %all_to_all.15 = f32[64,2,128]{2,1,0:T(2,128)} all-to-all(f32[64,2,128]{2,1,0:T(2,128)} %bitcast.7), channel_id=1, replica_groups=mesh['tile'=64,'agent'=8] {'tile'}, dimensions={0} | all-to-all | bytes 131072 | tf_op jit(solution)/shard_map/all_to_all | solution.py:232
  34.3 2.1 %residual.1 = f32[64,128]{1,0:T(8,128)} custom-call(f32[128,128]{1,0:T(8,128)} %bitcast.8), custom_call_target="tpu_custom_call" | custom-call | tf_op jit(solution)/shard_map/residual/pallas_call | solution.py:233
  36.4 17.5 %all_to_all.16 = f32[64,1,128]{2,1,0:T(1,128)} all-to-all(f32[64,1,128]{2,1,0:T(1,128)} %bitcast.10), channel_id=1, replica_groups=mesh['tile'=64,'agent'=8] {'tile'}, dimensions={0} | all-to-all | bytes 65536 | tf_op jit(solution)/shard_map/all_to_all | solution.py:240
  53.8 2.3 %gradient.1.reflect_ref = f32[8,8,512]{2,1,0:T(8,128)} custom-call(s32[8,1]{1,0:T(8,128)} %copy.11.offsets_ref, f32[64,128]{1,0:T(8,128)} %bitcast.9, f32[1,8,2,256]{3,2,1,0:T(2,128)} %states_ref.5, f32[8,1,64,512]{3,2,1,0:T(8,128)} %blocks_ref.3), custom_call_target="tpu_custom_call" | custom-call | tf_op jit(solution)/shard_map/gradient/pallas_call | solution.py:241
  56.1 9.9 %all-to-all-start.2 = ((f32[8,8,512]{2,1,0:T(8,128)}), f32[8,8,512]{2,1,0:T(8,128)S(1)}, u32[]{:S(2)}, u32[]{:S(2)}) async-start(f32[8,8,512]{2,1,0:T(8,128)} %gradient.1.reflect_ref), calls=%async_computation.2 | async-start | bytes 262144 | tf_op jit(solution)/shard_map/all_to_all | solution.py:248
  66.0 14.2 %all-to-all-done.2.in_ref = f32[8,8,512]{2,1,0:T(8,128)S(1)} async-done(((f32[8,8,512]{2,1,0:T(8,128)}), f32[8,8,512]{2,1,0:T(8,128)S(1)}, u32[]{:S(2)}, u32[]{:S(2)}) %all-to-all-start.2) | async-done | bytes 131104 | tf_op jit(solution)/shard_map/all_to_all | solution.py:248
  80.3 0.0 copy-start
  80.3 0.6 copy-done
  80.9 1.5 %mean.1.mean_ref = f32[8,512]{1,0:T(8,128)} custom-call(f32[8,8,512]{2,1,0:T(8,128)} %copy-done), custom_call_target="tpu_custom_call" | custom-call | tf_op jit(solution)/shard_map/mean/pallas_call | solution.py:249
  82.5 4.0 %collective-permute-start = (f32[8,512]{1,0:T(8,128)}, f32[8,512]{1,0:T(8,128)S(1)}, u32[]{:S(2)}, u32[]{:S(2)}) collective-permute-start(f32[8,512]{1,0:T(8,128)} %mean.1.mean_ref), channel_id=1, source_target_pairs={{0,8},{1,9},{2,10},{3,11},{4,12},{5,13},{6,14},{7,15},{8,0},{9,1},... | collective-permute-start | bytes 49160 | tf_op jit(solution)/shard_map/ppermute | solution.py:258
  86.5 5.0 %collective-permute-start.1 = (f32[8,512]{1,0:T(8,128)}, f32[8,512]{1,0:T(8,128)S(1)}, u32[]{:S(2)}, u32[]{:S(2)}) collective-permute-start(f32[8,512]{1,0:T(8,128)} %mean.1.mean_ref), channel_id=1, source_target_pairs={{8,16},{16,8},{9,17},{17,9},{10,18},{18,10},{11,19},{19,11},{12,20... | collective-permute-start | bytes 49160 | tf_op jit(solution)/shard_map/ppermute | solution.py:257
  91.5 0.6 pad_add_fusion.where_ref
  92.1 0.0 collective-permute-done.near_ref
  92.1 0.0 copy-start.1
  92.1 1.0 %collective-permute-done.1.side_ref = f32[8,512]{1,0:T(8,128)S(1)} collective-permute-done((f32[8,512]{1,0:T(8,128)}, f32[8,512]{1,0:T(8,128)S(1)}, u32[]{:S(2)}, u32[]{:S(2)}) %collective-permute-start.1) | collective-permute-done | bytes 16416 | tf_op jit(solution)/shard_map/ppermute | solution.py:257
  93.1 0.0 copy-done.1
  93.1 0.0 copy-start.2
  93.1 0.6 copy-done.2
  93.7 2.2 %prior.1 = (f32[1,8,2,256]{3,2,1,0:T(2,128)}, f32[8,2,256]{2,1,0:T(2,128)}) custom-call(s32[2]{0:T(128)} %pad_add_fusion.where_ref, f32[8,512]{1,0:T(8,128)} %mean.1.mean_ref, f32[8,512]{1,0:T(8,128)} %copy-done.1, f32[8,512]{1,0:T(8,128)} %copy-done.2, f32[1,8,2,256]{3,2,1,0:T(2,128)} %states_ref.5, f32[8,8,512]{2,1,0:T(8,128)} %gradient.1.reflect_ref), custom_call_target="tpu_custom_call" | custom-call | tf_op jit(solution)/shard_map/prior/pallas_call | solution.py:260
Async XLA Ops:
  56.1 24.2 %all-to-all-start.2 = ((f32[8,8,512]{2,1,0:T(8,128)}), f32[8,8,512]{2,1,0:T(8,128)S(1)}, u32[]{:S(2)}, u32[]{:S(2)}) async-start(f32[8,8,512]{2,1,0:T(8,128)} %gradient.1.reflect_ref), calls=%async_computation.2 | async-start | bytes 262144 | tf_op jit(solution)/shard_map/all_to_all | solution.py:248
  80.3 0.7 copy-start
  82.5 9.6 %collective-permute-start = (f32[8,512]{1,0:T(8,128)}, f32[8,512]{1,0:T(8,128)S(1)}, u32[]{:S(2)}, u32[]{:S(2)}) collective-permute-start(f32[8,512]{1,0:T(8,128)} %mean.1.mean_ref), channel_id=1, source_target_pairs={{0,8},{1,9},{2,10},{3,11},{4,12},{5,13},{6,14},{7,15},{8,0},{9,1},... | collective-permute-start | bytes 49160 | tf_op jit(solution)/shard_map/ppermute | solution.py:258
  86.5 6.6 %collective-permute-start.1 = (f32[8,512]{1,0:T(8,128)}, f32[8,512]{1,0:T(8,128)S(1)}, u32[]{:S(2)}, u32[]{:S(2)}) collective-permute-start(f32[8,512]{1,0:T(8,128)} %mean.1.mean_ref), channel_id=1, source_target_pairs={{8,16},{16,8},{9,17},{17,9},{10,18},{18,10},{11,19},{19,11},{12,20... | collective-permute-start | bytes 49160 | tf_op jit(solution)/shard_map/ppermute | solution.py:257
  92.1 1.0 %copy-start.1 = (f32[8,512]{1,0:T(8,128)}, f32[8,512]{1,0:T(8,128)S(1)}, u32[]{:S(2)}) copy-start(f32[8,512]{1,0:T(8,128)S(1)} %collective-permute-done.near_ref) | copy-start | bytes 49156
  93.1 0.6 copy-start.2

commit v2 on v1

--- a/solution.py
+++ b/solution.py
@@ -14,6 +14,14 @@
 
 SMEM = pl.BlockSpec(memory_space=pltpu.SMEM)
 VMEM = pl.BlockSpec(memory_space=pltpu.VMEM)
+
+
+def near(x):
+    return pltpu.with_memory_space_constraint(x, pltpu.VMEM)
+
+
+def near_shape(*shape):
+    return pltpu.VMEM(shape, jnp.float32)
 
 
 def neighbour_table():
@@ -60,7 +68,7 @@
     blank = jnp.zeros((slices, LANES - share), jnp.float32)
     for local in range(views):
         view = step * views + local
-        offset = offsets_ref[view, 0]
+        offset = offsets_ref[0, view]
         base = offset // BLOCK
         shift = offset - base * BLOCK
         at = (local % per_vreg) * foot
@@ -107,7 +115,7 @@
     per_vreg = LANES // foot
     pieces = []
     for view in range(views):
-        offset = offsets_ref[view, 0]
+        offset = offsets_ref[0, view]
         shift = offset - (offset // BLOCK) * BLOCK
         at = (view % per_vreg) * foot
         window = windows_ref[view * slices : (view + 1) * slices, :]
@@ -167,10 +175,10 @@
     return out
 
 
-def prior_kernel(where_ref, mean_ref, near_ref, side_ref, states_ref, reflect_ref, new_ref, prior_ref):
+def prior_kernel(mean_ref, near_ref, side_ref, states_ref, reflect_ref, new_ref, prior_ref):
     width = states_ref.shape[3]
-    tile = where_ref[0]
-    last = where_ref[1]
+    tile = lax.axis_index("tile")
+    last = lax.axis_size("tile") - 1
     odd = tile % 2 == 1
     near = near_ref[...]
     side = side_ref[...]
@@ -215,6 +223,7 @@
     f32 = jnp.float32
 
     half = views // 2
+    starts = offsets.reshape(1, views)
     sent = pl.pallas_call(
         project_kernel,
         grid=(2,),
@@ -226,58 +235,47 @@
             pl.BlockSpec((half, slices, share), lambda i: (i, 0, 0)),
         ],
         out_specs=pl.BlockSpec((2 * n_tile, LANES), lambda i: (0, 0)),
-        out_shape=jax.ShapeDtypeStruct((2 * n_tile, LANES), f32),
+        out_shape=near_shape(2 * n_tile, LANES),
         name="project",
-    )(offsets, states, footprints, measured, weights)
+    )(starts, states, footprints, measured, weights)
     bands = lax.all_to_all(sent.reshape(n_tile, 2, LANES), "tile", 0, 0, tiled=True)
     back = pl.pallas_call(
         residual_kernel,
         in_specs=[VMEM],
         out_specs=VMEM,
-        out_shape=jax.ShapeDtypeStruct((n_tile, LANES), f32),
+        out_shape=near_shape(n_tile, LANES),
         name="residual",
-    )(bands.reshape(2 * n_tile, LANES))
+    )(near(bands.reshape(2 * n_tile, LANES)))
     windows = lax.all_to_all(back.reshape(n_tile, 1, LANES), "tile", 0, 0, tiled=True)
+    states_near = near(states)
     copies = pl.pallas_call(
         gradient_kernel,
         in_specs=[SMEM, VMEM, VMEM, VMEM],
         out_specs=VMEM,
-        out_shape=jax.ShapeDtypeStruct((n_agent, slices, pixels), f32),
+        out_shape=near_shape(n_agent, slices, pixels),
         name="gradient",
-    )(offsets, windows.reshape(n_tile, LANES), states, footprints)
+    )(starts, near(windows.reshape(n_tile, LANES)), states_near, near(footprints))
     reflects = lax.all_to_all(copies, "agent", 0, 0, tiled=True)
     mean = pl.pallas_call(
         mean_kernel,
         in_specs=[VMEM],
         out_specs=VMEM,
-        out_shape=jax.ShapeDtypeStruct((slices, pixels), f32),
+        out_shape=near_shape(slices, pixels),
         name="mean",
-    )(reflects)
-    near_pairs, side_pairs = halo_pairs(n_tile, n_agent, 16)
+    )(near(reflects))
+    core_pairs, side_pairs = halo_pairs(n_tile, n_agent, 16)
     side = lax.ppermute(mean, ("tile", "agent"), side_pairs)
-    near = lax.ppermute(mean, ("tile", "agent"), near_pairs)
-    where = jnp.stack([lax.axis_index("tile"), jnp.int32(n_tile - 1)]).astype(jnp.int32)
+    core = lax.ppermute(mean, ("tile", "agent"), core_pairs)
     new_states, prior = pl.pallas_call(
         prior_kernel,
-        grid=(1,),
-        in_specs=[
-            SMEM,
-            pl.BlockSpec((slices, pixels), lambda i: (0, 0)),
-            pl.BlockSpec((slices, pixels), lambda i: (0, 0)),
-            pl.BlockSpec((slices, pixels), lambda i: (0, 0)),
-            pl.BlockSpec(states.shape, lambda i: (0, 0, 0, 0)),
-            pl.BlockSpec((1, slices, pixels), lambda i: (0, 0, 0)),
-        ],
-        out_specs=[
-            pl.BlockSpec(states.shape, lambda i: (0, 0, 0, 0)),
-            pl.BlockSpec((slices, height, width), lambda i: (0, 0, 0)),
-        ],
+        in_specs=[VMEM] * 5,
+        out_specs=[VMEM, VMEM],
         out_shape=[
             jax.ShapeDtypeStruct(states.shape, f32),
             jax.ShapeDtypeStruct((slices, height, width), f32),
         ],
         name="prior",
-    )(where, mean, near, side, states, copies)
+    )(near(mean), near(core), near(side), states_near, near(copies))
     return new_states, prior
 
 

time: 96.4 us -> 87 us (0.902)
  blocking collectives: 47.4 us -> 70.9 us
  waiting for transfers between devices: 15.3 us -> 1.14 us
  starting transfers between devices: 18.9 us -> 9.11 us
  Pallas kernels: 10.4 us -> 4.86 us
  local copies, waits for them, and re-layouts: 2.57 us -> 0.01 us
    all_to_all x0 -> x1, blocking collectives: none -> 24 us  [shards(): reflects = lax.all_to_all(copies, 'agent', 0, 0, tiled=True)]
    all_to_all x1 -> x0, waiting for transfers between devices: 14.2 us -> none  [shards(): reflects = lax.all_to_all(copies, 'agent', 0, 0, tiled=True)]
    all_to_all x1 -> x0, starting transfers between devices: 9.94 us -> none  [shards(): reflects = lax.all_to_all(copies, 'agent', 0, 0, tiled=True)]
    unnamed x7 -> x4, local copies, waits for them, and re-layouts: 2.57 us -> 0.01 us
    pallas_call x2, Pallas kernels: 3.69 us -> 1.4 us  [the longest x1 1.38 us: shards(): pl.pallas_call(prior_kernel, in_specs=[VMEM] * 5, out_specs=[VMEM, VMEM],...]
    ppermute x1, starting transfers between devices: 4.97 us -> 7.19 us  [shards(): side = lax.ppermute(mean, ('tile', 'agent'), side_pairs)]
    ppermute x1, starting transfers between devices: 4.04 us -> 1.92 us  [shards(): core = lax.ppermute(mean, ('tile', 'agent'), core_pairs)]
    pallas_call x1, Pallas kernels: 2.11 us -> 0.64 us  [shards(): pl.pallas_call(residual_kernel, in_specs=[VMEM], out_specs=VMEM, out_shap...]
  transfers between devices with their start and end apart: 3 -> 2, of which waited for: 2 -> 1; matrix products, arithmetic and copies ran while one was open for 1% -> 0% of each run, Pallas kernels for 0% -> 0%
where the time goes in v2:
time: 87 us; the launch traced here: 86.7 us
  blocking collectives  70.9 us (81%)
  starting transfers between devices  9.11 us (10%)
  Pallas kernels  4.86 us (6%)
  waiting for transfers between devices  1.14 us (1%)
    all_to_all x1, blocking collectives, shards(): lax.all_to_all(sent.reshape(n_tile, 2, LANES), 'tile', 0, 0, tiled=True)  29.6 us
    all_to_all x1, blocking collectives, shards(): reflects = lax.all_to_all(copies, 'agent', 0, 0, tiled=True)  24 us
    all_to_all x1, blocking collectives, shards(): lax.all_to_all(back.reshape(n_tile, 1, LANES), 'tile', 0, 0, tiled=True)  17.2 us
    ppermute x1, starting transfers between devices, shards(): side = lax.ppermute(mean, ('tile', 'agent'), side_pairs)  7.19 us
    ppermute x1, starting transfers between devices, shards(): core = lax.ppermute(mean, ('tile', 'agent'), core_pairs)  1.92 us
    pallas_call x1, Pallas kernels, shards(): pl.pallas_call(project_kernel, grid=(2,), in_specs=[SMEM, pl.BlockSpec(st...  1.82 us
  transfers between devices with their start and end apart: 2, of which 1 were waited for; matrix products, arithmetic and copies ran while one was open for 0% of the time, Pallas kernels for 0%

profile of v2, /device:TPU:1, one launch (start us, length us, event | category | flops | bytes accessed | tf_op | source)
XLA Modules:
  0.0 86.7 jit_solution(16773556996173534051)
XLA Ops:
  0.6 0.0 copy-start
  0.6 1.8 %project.1 = f32[128,128]{1,0:T(8,128)S(1)} custom-call(s32[1,8]{1,0:T(1,128)} %bitcast.11, f32[1,8,2,256]{3,2,1,0:T(2,128)} %states_ref.5, f32[8,1,64,512]{3,2,1,0:T(8,128)} %blocks_ref.3, f32[8,8,32]{2,1,0:T(8,128)} %measured_ref.1, f32[8,8,32]{2,1,0:T(8,128)} %weights_ref.1), custom_call_target="tpu_custom_call" | custom-call | tf_op jit(solution)/shard_map/project/pallas_call | solution.py:227
  2.5 29.6 %all_to_all.15 = f32[64,2,128]{2,1,0:T(2,128)S(1)} all-to-all(f32[64,2,128]{2,1,0:T(2,128)S(1)} %bitcast.7), channel_id=1, replica_groups=mesh['tile'=64,'agent'=8] {'tile'}, dimensions={0} | all-to-all | bytes 131072 | tf_op jit(solution)/shard_map/all_to_all | solution.py:241
  32.1 0.6 residual.1
  32.8 0.0 copy-start.1
  32.8 17.2 %all_to_all.16 = f32[64,1,128]{2,1,0:T(1,128)S(1)} all-to-all(f32[64,1,128]{2,1,0:T(1,128)S(1)} %bitcast.9), channel_id=1, replica_groups=mesh['tile'=64,'agent'=8] {'tile'}, dimensions={0} | all-to-all | bytes 65536 | tf_op jit(solution)/shard_map/all_to_all | solution.py:249
  50.0 0.0 copy-done
  50.0 0.0 copy-done.1
  50.0 1.0 %gradient.1.reflect_ref = f32[8,8,512]{2,1,0:T(8,128)S(1)} custom-call(s32[1,8]{1,0:T(1,128)} %bitcast.12, f32[64,128]{1,0:T(8,128)S(1)} %bitcast.10, f32[1,8,2,256]{3,2,1,0:T(2,128)S(1)} %copy-done.1, f32[8,1,64,512]{3,2,1,0:T(8,128)S(1)} %copy-done), custom_call_target="tpu_custom_call" | custom-call | tf_op jit(solution)/shard_map/gradient/pallas_call | solution.py:251
  51.0 24.0 %all_to_all.17.in_ref = f32[8,8,512]{2,1,0:T(8,128)S(1)} all-to-all(f32[8,8,512]{2,1,0:T(8,128)S(1)} %gradient.1.reflect_ref), channel_id=1, replica_groups=mesh['tile'=64,'agent'=8] {'agent'}, dimensions={0} | all-to-all | bytes 262144 | tf_op jit(solution)/shard_map/all_to_all | solution.py:258
  75.0 7.2 %collective-permute-start.1 = (f32[8,512]{1,0:T(8,128)S(1)}, f32[8,512]{1,0:T(8,128)S(1)}, u32[]{:S(2)}, u32[]{:S(2)}) collective-permute-start(f32[8,512]{1,0:T(8,128)S(1)} %mean.1.mean_ref), channel_id=1, source_target_pairs={{8,16},{16,8},{9,17},{17,9},{10,18},{18,10},{11,19},{19,11},{12,20... | collective-permute-start | bytes 49160 | tf_op jit(solution)/shard_map/ppermute | solution.py:267
  82.2 1.9 %collective-permute-start = (f32[8,512]{1,0:T(8,128)S(1)}, f32[8,512]{1,0:T(8,128)S(1)}, u32[]{:S(2)}, u32[]{:S(2)}) collective-permute-start(f32[8,512]{1,0:T(8,128)S(1)} %mean.1.mean_ref), channel_id=1, source_target_pairs={{0,8},{1,9},{2,10},{3,11},{4,12},{5,13},{6,14},{7,15},{8,0},{9,1},... | collective-permute-start | bytes 49160 | tf_op jit(solution)/shard_map/ppermute | solution.py:268
  84.1 0.0 collective-permute-done.1.side_ref
  84.1 1.1 %collective-permute-done.near_ref = f32[8,512]{1,0:T(8,128)S(1)} collective-permute-done((f32[8,512]{1,0:T(8,128)S(1)}, f32[8,512]{1,0:T(8,128)S(1)}, u32[]{:S(2)}, u32[]{:S(2)}) %collective-permute-start) | collective-permute-done | bytes 16416 | tf_op jit(solution)/shard_map/ppermute | solution.py:268
  85.3 1.4 %prior.1 = (f32[1,8,2,256]{3,2,1,0:T(2,128)}, f32[8,2,256]{2,1,0:T(2,128)}) custom-call(f32[8,512]{1,0:T(8,128)S(1)} %mean.1.mean_ref, f32[8,512]{1,0:T(8,128)S(1)} %collective-permute-done.near_ref, f32[8,512]{1,0:T(8,128)S(1)} %collective-permute-done.1.side_ref, f32[1,8,2,256]{3,2,1,0:T(2,128)S(1)} %copy-done.1, f32[8,8,512]{2,1,0:T(8,128)S(1)} %gradient.1.reflect_ref), custom_call_target="tpu_custom_call" | custom-call | tf_op jit(solution)/shard_map/prior/pallas_call | solution.py:269
  (1 shorter events, 0.0 us)
Async XLA Ops:
  0.6 49.4 %copy-start = (f32[8,1,64,512]{3,2,1,0:T(8,128)S(1)}, f32[8,1,64,512]{3,2,1,0:T(8,128)}, u32[]{:S(2)}) copy-start(f32[8,1,64,512]{3,2,1,0:T(8,128)} %blocks_ref.3) | copy-start | bytes 3145732
  32.8 17.2 %copy-start.1 = (f32[1,8,2,256]{3,2,1,0:T(2,128)S(1)}, f32[1,8,2,256]{3,2,1,0:T(2,128)}, u32[]{:S(2)}) copy-start(f32[1,8,2,256]{3,2,1,0:T(2,128)} %states_ref.5) | copy-start | bytes 49156
  75.0 9.1 %collective-permute-start.1 = (f32[8,512]{1,0:T(8,128)S(1)}, f32[8,512]{1,0:T(8,128)S(1)}, u32[]{:S(2)}, u32[]{:S(2)}) collective-permute-start(f32[8,512]{1,0:T(8,128)S(1)} %mean.1.mean_ref), channel_id=1, source_target_pairs={{8,16},{16,8},{9,17},{17,9},{10,18},{18,10},{11,19},{19,11},{12,20... | collective-permute-start | bytes 49160 | tf_op jit(solution)/shard_map/ppermute | solution.py:267
  82.2 3.1 %collective-permute-start = (f32[8,512]{1,0:T(8,128)S(1)}, f32[8,512]{1,0:T(8,128)S(1)}, u32[]{:S(2)}, u32[]{:S(2)}) collective-permute-start(f32[8,512]{1,0:T(8,128)S(1)} %mean.1.mean_ref), channel_id=1, source_target_pairs={{0,8},{1,9},{2,10},{3,11},{4,12},{5,13},{6,14},{7,15},{8,0},{9,1},... | collective-permute-start | bytes 49160 | tf_op jit(solution)/shard_map/ppermute | solution.py:268

commit v3 on v2

--- a/solution.py
+++ b/solution.py
@@ -110,7 +110,6 @@
 def gradient_kernel(offsets_ref, windows_ref, states_ref, blocks_ref, out_ref):
     views, _, foot, pixels = blocks_ref.shape
     slices, width = states_ref.shape[1], states_ref.shape[3]
-    copies = out_ref.shape[0]
     lane = lane_iota((slices, LANES))
     per_vreg = LANES // foot
     pieces = []
@@ -129,17 +128,26 @@
     gradient = split_dot(windows, blocks, ((1,), (0,)))
     for row in range(2):
         at = slice(row * width, (row + 1) * width)
-        reflect = states_ref[0, :, row, :] - (2.0 * STEP_SIZE) * gradient[:, at]
-        for copy in range(copies):
-            out_ref[copy, :, at] = reflect
-
-
-def mean_kernel(in_ref, out_ref):
-    count = in_ref.shape[0]
-    total = in_ref[0]
-    for agent in range(1, count):
-        total = total + in_ref[agent]
-    out_ref[...] = total * (1.0 / count)
+        out_ref[:, at] = states_ref[0, :, row, :] - (2.0 * STEP_SIZE) * gradient[:, at]
+
+
+def pair_kernel(in_ref, out_ref):
+    total = in_ref[0] + in_ref[1]
+    for copy in range(out_ref.shape[0]):
+        out_ref[copy] = total
+
+
+def mean_kernel(in_ref, own_ref, other_ref):
+    count = in_ref.shape[0] // 2
+    means = []
+    for half in range(2):
+        total = in_ref[half * count]
+        for member in range(1, count):
+            total = total + in_ref[half * count + member]
+        means.append(total * (0.5 / count))
+    odd = lax.axis_index("tile") % 2 == 1
+    own_ref[...] = jnp.where(odd, means[1], means[0])
+    other_ref[...] = jnp.where(odd, means[0], means[1])
 
 
 def shifted(row, a, c):
@@ -194,24 +202,30 @@
     swept[3] = jnp.where(tile == last, 0.0, swept[3])
     final = sweep_rows(swept, averages[2:4])
     for row in range(2):
-        reflect = reflect_ref[0, :, row * width : (row + 1) * width]
+        reflect = reflect_ref[:, row * width : (row + 1) * width]
         prior_ref[:, row, :] = final[row]
         new_ref[0, :, row, :] = (1.0 - RELAX) * states_ref[0, :, row, :] + RELAX * (2.0 * final[row] - reflect)
 
 
-def halo_pairs(n_tile, n_agent, per_x):
-    near, side = [], []
-    for tile in range(n_tile):
-        for agent in range(n_agent):
-            near.append((tile * n_agent + agent, (tile ^ 1) * n_agent + agent))
+def side_pairs(n_tile, n_agent, per_x):
+    pairs = []
     for tile in range(1, n_tile - 1, 2):
         other = tile + 1
         for agent in range(n_agent):
             crossing = tile // per_x != other // per_x
             partner = (agent + n_agent // 2) % n_agent if crossing else agent
             one, two = tile * n_agent + agent, other * n_agent + partner
-            side += [(one, two), (two, one)]
-    return near, side
+            pairs += [(one, two), (two, one)]
+    return pairs
+
+
+def chip_groups(n_tile, n_agent):
+    half = n_agent // 2
+    return [
+        [(tile + core) * n_agent + first + y for core in range(2) for y in range(half)]
+        for tile in range(0, n_tile, 2)
+        for first in (0, half)
+    ]
 
 
 def shards(states, footprints, offsets, measured, weights):
@@ -248,24 +262,32 @@
     )(near(bands.reshape(2 * n_tile, LANES)))
     windows = lax.all_to_all(back.reshape(n_tile, 1, LANES), "tile", 0, 0, tiled=True)
     states_near = near(states)
-    copies = pl.pallas_call(
+    reflect = pl.pallas_call(
         gradient_kernel,
         in_specs=[SMEM, VMEM, VMEM, VMEM],
         out_specs=VMEM,
-        out_shape=near_shape(n_agent, slices, pixels),
+        out_shape=near_shape(slices, pixels),
         name="gradient",
     )(starts, near(windows.reshape(n_tile, LANES)), states_near, near(footprints))
-    reflects = lax.all_to_all(copies, "agent", 0, 0, tiled=True)
-    mean = pl.pallas_call(
+    half = n_agent // 2
+    both = lax.all_gather(reflect, "agent", axis=0, axis_index_groups=[[y, half + y] for y in range(half)])
+    copies = pl.pallas_call(
+        pair_kernel,
+        in_specs=[VMEM],
+        out_specs=VMEM,
+        out_shape=near_shape(n_agent, slices, pixels),
+        name="pair",
+    )(near(both))
+    axes = ("tile", "agent")
+    shares = lax.all_to_all(copies, axes, 0, 0, tiled=True, axis_index_groups=chip_groups(n_tile, n_agent))
+    mean, core = pl.pallas_call(
         mean_kernel,
         in_specs=[VMEM],
-        out_specs=VMEM,
-        out_shape=near_shape(slices, pixels),
+        out_specs=[VMEM, VMEM],
+        out_shape=[near_shape(slices, pixels), near_shape(slices, pixels)],
         name="mean",
-    )(near(reflects))
-    core_pairs, side_pairs = halo_pairs(n_tile, n_agent, 16)
-    side = lax.ppermute(mean, ("tile", "agent"), side_pairs)
-    core = lax.ppermute(mean, ("tile", "agent"), core_pairs)
+    )(near(shares))
+    side = lax.ppermute(mean, axes, side_pairs(n_tile, n_agent, 16))
     new_states, prior = pl.pallas_call(
         prior_kernel,
         in_specs=[VMEM] * 5,
@@ -275,7 +297,7 @@
             jax.ShapeDtypeStruct((slices, height, width), f32),
         ],
         name="prior",
-    )(near(mean), near(core), near(side), states_near, near(copies))
+    )(near(mean), near(core), near(side), states_near, near(reflect))
     return new_states, prior
 
 

time: 87 us -> 81.2 us (0.933)
  starting transfers between devices: 9.11 us -> 2.59 us
  waiting for transfers between devices: 1.14 us -> 2.46 us
    all_to_all x1, blocking collectives: 24 us -> 11.3 us  [shards(): lax.all_to_all(copies, axes, 0, 0, tiled=True, axis_index_groups=chip_gro...]
    all_gather x0 -> x1, blocking collectives: none -> 12 us  [shards(): lax.all_gather(reflect, 'agent', axis=0, axis_index_groups=[[y, half + y]...]
    ppermute x2 -> x1, starting transfers between devices: 9.11 us -> 2.59 us  [shards(): side = lax.ppermute(mean, axes, side_pairs(n_tile, n_agent, 16))]
    ppermute x2 -> x1, waiting for transfers between devices: 1.14 us -> 2.46 us  [shards(): side = lax.ppermute(mean, axes, side_pairs(n_tile, n_agent, 16))]
  transfers between devices with their start and end apart: 2 -> 1, of which waited for: 1 -> 1; matrix products, arithmetic and copies ran while one was open for 0% -> 0% of each run, Pallas kernels for 0% -> 0%
where the time goes in v3:
time: 81.2 us; the launch traced here: 80.7 us
  blocking collectives  70.1 us (86%)
  Pallas kernels  4.87 us (6%)
  starting transfers between devices  2.59 us (3%)
  waiting for transfers between devices  2.46 us (3%)
    all_to_all x1, blocking collectives, shards(): lax.all_to_all(sent.reshape(n_tile, 2, LANES), 'tile', 0, 0, tiled=True)  29.6 us
    all_to_all x1, blocking collectives, shards(): lax.all_to_all(back.reshape(n_tile, 1, LANES), 'tile', 0, 0, tiled=True)  17.2 us
    all_gather x1, blocking collectives, shards(): lax.all_gather(reflect, 'agent', axis=0, axis_index_groups=[[y, half + y]...  12 us
    all_to_all x1, blocking collectives, shards(): lax.all_to_all(copies, axes, 0, 0, tiled=True, axis_index_groups=chip_gro...  11.3 us
    ppermute x1, starting transfers between devices, shards(): side = lax.ppermute(mean, axes, side_pairs(n_tile, n_agent, 16))  2.59 us
    ppermute x1, waiting for transfers between devices, shards(): side = lax.ppermute(mean, axes, side_pairs(n_tile, n_agent, 16))  2.46 us
    pallas_call x1, Pallas kernels, shards(): pl.pallas_call(project_kernel, grid=(2,), in_specs=[SMEM, pl.BlockSpec(st...  1.82 us
  transfers between devices with their start and end apart: 1, of which 1 were waited for; matrix products, arithmetic and copies ran while one was open for 0% of the time, Pallas kernels for 0%

profile of v3, /device:TPU:1, one launch (start us, length us, event | category | flops | bytes accessed | tf_op | source)
XLA Modules:
  0.0 80.7 jit_solution(11963668781581571059)
XLA Ops:
  0.6 0.0 copy-start
  0.6 1.8 %project.1 = f32[128,128]{1,0:T(8,128)S(1)} custom-call(s32[1,8]{1,0:T(1,128)} %bitcast.13, f32[1,8,2,256]{3,2,1,0:T(2,128)} %states_ref.5, f32[8,1,64,512]{3,2,1,0:T(8,128)} %blocks_ref.3, f32[8,8,32]{2,1,0:T(8,128)} %measured_ref.1, f32[8,8,32]{2,1,0:T(8,128)} %weights_ref.1), custom_call_target="tpu_custom_call" | custom-call | tf_op jit(solution)/shard_map/project/pallas_call | solution.py:241
  2.5 29.6 %all_to_all.15 = f32[64,2,128]{2,1,0:T(2,128)S(1)} all-to-all(f32[64,2,128]{2,1,0:T(2,128)S(1)} %bitcast.8), channel_id=1, replica_groups=mesh['tile'=64,'agent'=8] {'tile'}, dimensions={0} | all-to-all | bytes 131072 | tf_op jit(solution)/shard_map/all_to_all | solution.py:255
  32.1 0.6 residual.1
  32.8 0.0 copy-start.1
  32.8 17.2 %all_to_all.16 = f32[64,1,128]{2,1,0:T(1,128)S(1)} all-to-all(f32[64,1,128]{2,1,0:T(1,128)S(1)} %bitcast.10), channel_id=1, replica_groups=mesh['tile'=64,'agent'=8] {'tile'}, dimensions={0} | all-to-all | bytes 65536 | tf_op jit(solution)/shard_map/all_to_all | solution.py:263
  50.0 0.0 copy-done
  50.0 0.0 copy-done.1
  50.0 1.0 %gradient.1.reflect_ref = f32[8,512]{1,0:T(8,128)S(1)} custom-call(s32[1,8]{1,0:T(1,128)} %bitcast.14, f32[64,128]{1,0:T(8,128)S(1)} %bitcast.11, f32[1,8,2,256]{3,2,1,0:T(2,128)S(1)} %copy-done.1, f32[8,1,64,512]{3,2,1,0:T(8,128)S(1)} %copy-done), custom_call_target="tpu_custom_call" | custom-call | tf_op jit(solution)/shard_map/gradient/pallas_call | solution.py:265
  51.0 12.0 %all-gather = f32[16,512]{1,0:T(8,128)S(1)} all-gather(f32[8,512]{1,0:T(8,128)S(1)} %gradient.1.reflect_ref), channel_id=2, replica_groups={{0,4},{1,5},{2,6},{3,7},{8,12},{9,13},{10,14},{11,15},{16,20},{17,21},{..., dimensions={0}, use_global_device_ids=true | all-gather | bytes 49152 | tf_op jit(solution)/shard_map/all_gather | solution.py:273
  63.0 11.3 %all_to_all.17.in_ref = f32[8,8,512]{2,1,0:T(8,128)S(1)} all-to-all(f32[8,8,512]{2,1,0:T(8,128)S(1)} %pair.1), channel_id=1, replica_groups={{0,1,2,3,8,9,10,11},{4,5,6,7,12,13,14,15},{16,17,18,19,24,25,26,27},{20..., dimensions={0} | all-to-all | bytes 262144 | tf_op jit(solution)/shard_map/all_to_all | solution.py:282
  74.2 2.6 %collective-permute-start = (f32[8,512]{1,0:T(8,128)S(1)}, f32[8,512]{1,0:T(8,128)S(1)}, u32[]{:S(2)}, u32[]{:S(2)}) collective-permute-start(f32[8,512]{1,0:T(8,128)S(1)} %get-tuple-element.4.mean_ref), channel_id=1, source_target_pairs={{8,16},{16,8},{9,17},{17,9},{10,18},{18,10},{11,19},{19,11},{12,20... | collective-permute-start | bytes 49160 | tf_op jit(solution)/shard_map/ppermute | solution.py:290
  76.8 2.5 %collective-permute-done.side_ref = f32[8,512]{1,0:T(8,128)S(1)} collective-permute-done((f32[8,512]{1,0:T(8,128)S(1)}, f32[8,512]{1,0:T(8,128)S(1)}, u32[]{:S(2)}, u32[]{:S(2)}) %collective-permute-start) | collective-permute-done | bytes 16416 | tf_op jit(solution)/shard_map/ppermute | solution.py:290
  79.3 1.4 %prior.1 = (f32[1,8,2,256]{3,2,1,0:T(2,128)}, f32[8,2,256]{2,1,0:T(2,128)}) custom-call(f32[8,512]{1,0:T(8,128)S(1)} %get-tuple-element.4.mean_ref, f32[8,512]{1,0:T(8,128)S(1)} %get-tuple-element.5.near_ref, f32[8,512]{1,0:T(8,128)S(1)} %collective-permute-done.side_ref, f32[1,8,2,256]{3,2,1,0:T(2,128)S(1)} %copy-done.1, f32[8,512]{1,0:T(8,128)S(1)} %gradient.1.reflect_ref), custom_call_target="tpu_custom_call" | custom-call | tf_op jit(solution)/shard_map/prior/pallas_call | solution.py:291
  (2 shorter events, 0.0 us)
Async XLA Ops:
  0.6 49.4 %copy-start = (f32[8,1,64,512]{3,2,1,0:T(8,128)S(1)}, f32[8,1,64,512]{3,2,1,0:T(8,128)}, u32[]{:S(2)}) copy-start(f32[8,1,64,512]{3,2,1,0:T(8,128)} %blocks_ref.3) | copy-start | bytes 3145732
  32.8 17.2 %copy-start.1 = (f32[1,8,2,256]{3,2,1,0:T(2,128)S(1)}, f32[1,8,2,256]{3,2,1,0:T(2,128)}, u32[]{:S(2)}) copy-start(f32[1,8,2,256]{3,2,1,0:T(2,128)} %states_ref.5) | copy-start | bytes 49156
  74.2 5.1 %collective-permute-start = (f32[8,512]{1,0:T(8,128)S(1)}, f32[8,512]{1,0:T(8,128)S(1)}, u32[]{:S(2)}, u32[]{:S(2)}) collective-permute-start(f32[8,512]{1,0:T(8,128)S(1)} %get-tuple-element.4.mean_ref), channel_id=1, source_target_pairs={{8,16},{16,8},{9,17},{17,9},{10,18},{18,10},{11,19},{19,11},{12,20... | collective-permute-start | bytes 49160 | tf_op jit(solution)/shard_map/ppermute | solution.py:290

commit v4 on v3

--- a/solution.py
+++ b/solution.py
@@ -8,12 +8,12 @@
 SWEEPS = 2
 STEP_SIZE = 0.25
 RELAX = 0.6
-QRATIO = 0.6
 BLOCK = 32
 LANES = 128
 
 SMEM = pl.BlockSpec(memory_space=pltpu.SMEM)
 VMEM = pl.BlockSpec(memory_space=pltpu.VMEM)
+ANY = pl.BlockSpec(memory_space=pl.ANY)
 
 
 def near(x):
@@ -55,32 +55,78 @@
     return lax.broadcasted_iota(jnp.int32, shape, len(shape) - 1)
 
 
-def project_kernel(offsets_ref, states_ref, blocks_ref, measured_ref, weights_ref, out_ref):
+PIECES = 4
+
+
+def project_kernel(
+    offsets_ref, states_hbm, blocks_hbm, measured_hbm, weights_hbm, out_ref, blocks_ref,
+    states_ref, measured_ref, weights_ref, piece_sems, small_sems,
+):
     views, _, foot, pixels = blocks_ref.shape
     slices, width = states_ref.shape[1], states_ref.shape[3]
     share = measured_ref.shape[2]
+    per_piece = views // PIECES
+    small = [
+        pltpu.make_async_copy(source, target, small_sems.at[i])
+        for i, (source, target) in enumerate(
+            ((states_hbm, states_ref), (measured_hbm, measured_ref), (weights_hbm, weights_ref))
+        )
+    ]
+    pieces = [
+        pltpu.make_async_copy(
+            blocks_hbm.at[pl.ds(i * per_piece, per_piece)], blocks_ref.at[pl.ds(i * per_piece, per_piece)], piece_sems.at[i]
+        )
+        for i in range(PIECES)
+    ]
+    small[0].start()
+    pieces[0].start()
+    small[1].start()
+    small[2].start()
+    for piece in pieces[1:]:
+        piece.start()
     lane = lane_iota((slices, LANES))
-    blocks = blocks_ref[:, 0].reshape(views * foot, pixels)
-    projected = split_dot(states_ref[0, :, 0, :], blocks[:, :width], ((1,), (1,)))
-    projected += split_dot(states_ref[0, :, 1, :], blocks[:, width:], ((1,), (1,)))
-    step = pl.program_id(0)
     per_vreg = LANES // foot
     blank = jnp.zeros((slices, LANES - share), jnp.float32)
-    for local in range(views):
-        view = step * views + local
-        offset = offsets_ref[0, view]
-        base = offset // BLOCK
-        shift = offset - base * BLOCK
-        at = (local % per_vreg) * foot
-        pair = projected[:, (local // per_vreg) * LANES : (local // per_vreg + 1) * LANES]
-        band = jnp.where((lane >= at) & (lane < at + foot), pair, 0.0)
-        band = pltpu.roll(band, (shift + LANES - at) % LANES, 1)
-        first = band + jnp.concatenate([blank, measured_ref[local]], axis=1)
-        second = jnp.concatenate([weights_ref[local], blank], axis=1)
-        second = jnp.where(lane == share, base.astype(jnp.float32), second)
-        start = view * 2 * slices
-        out_ref[pl.ds(start, slices, stride=2), :] = first
-        out_ref[pl.ds(start + 1, slices, stride=2), :] = second
+    for index, piece in enumerate(pieces):
+        if index == 0:
+            small[0].wait()
+        piece.wait()
+        first_view = index * per_piece
+        blocks = blocks_ref[first_view : first_view + per_piece, 0].reshape(per_piece * foot, pixels)
+        projected = split_dot(states_ref[0, :, 0, :], blocks[:, :width], ((1,), (1,)))
+        projected += split_dot(states_ref[0, :, 1, :], blocks[:, width:], ((1,), (1,)))
+        if index == 0:
+            small[1].wait()
+            small[2].wait()
+        for local in range(per_piece):
+            view = first_view + local
+            offset = offsets_ref[0, view]
+            base = offset // BLOCK
+            shift = offset - base * BLOCK
+            at = (local % per_vreg) * foot
+            pair = projected[:, (local // per_vreg) * LANES : (local // per_vreg + 1) * LANES]
+            band = jnp.where((lane >= at) & (lane < at + foot), pair, 0.0)
+            band = pltpu.roll(band, (shift + LANES - at) % LANES, 1)
+            first = band + jnp.concatenate([blank, measured_ref[view]], axis=1)
+            second = jnp.concatenate([weights_ref[view], blank], axis=1)
+            second = jnp.where(lane == share, base.astype(jnp.float32), second)
+            start = view * 2 * slices
+            out_ref[pl.ds(start, slices, stride=2), :] = first
+            out_ref[pl.ds(start + 1, slices, stride=2), :] = second
+
+
+def thirds(x):
+    high = x.astype(jnp.bfloat16)
+    rest = x - high.astype(jnp.float32)
+    mid = rest.astype(jnp.bfloat16)
+    low = (rest - mid.astype(jnp.float32)).astype(jnp.bfloat16)
+    return jnp.concatenate([high, mid, low], axis=1)
+
+
+def select_dot(onehot, x, dims):
+    width = x.shape[1]
+    all_three = lax.dot_general(onehot, thirds(x), (dims, ((), ())), preferred_element_type=jnp.float32)
+    return all_three[:, :width] + (all_three[:, width : 2 * width] + all_three[:, 2 * width :])
 
 
 def residual_kernel(in_ref, out_ref):
@@ -90,10 +136,8 @@
     first = in_ref[pl.ds(0, tiles, stride=2), :]
     second = in_ref[pl.ds(1, tiles, stride=2), :]
     base = second[:, share : share + 1].astype(jnp.int32)
-    onehot = jnp.where(lane_iota((tiles, tiles)) == base, 1.0, 0.0)
-    placed = lax.dot_general(
-        onehot, first, (((0,), (0,)), ((), ())), precision=lax.Precision.HIGHEST, preferred_element_type=jnp.float32
-    )
+    onehot = jnp.where(lane_iota((tiles, tiles)) == base, 1.0, 0.0).astype(jnp.bfloat16)
+    placed = select_dot(onehot, first, ((0,), (0,)))
     total = placed
     for part in (1, 2):
         moved = pltpu.roll(placed, part, 0)
@@ -104,7 +148,7 @@
     for part in (1, 2):
         moved = pltpu.roll(residual, tiles - part, 0)
         windows += pltpu.roll(moved, part * share, 1)
-    out_ref[...] = jnp.dot(onehot, windows, precision=lax.Precision.HIGHEST, preferred_element_type=jnp.float32)
+    out_ref[...] = select_dot(onehot, windows, ((1,), (0,)))
 
 
 def gradient_kernel(offsets_ref, windows_ref, states_ref, blocks_ref, out_ref):
@@ -169,16 +213,20 @@
     out = []
     for index, average in enumerate(averages):
         centre = rows[index + 1]
-        numerator = average
-        denominator = jnp.ones_like(average)
+        above, below = {}, {}
         for a, b, c, weight_nb in table:
             neighbour = moved[index + 1 + b][(a, c)]
             differ = centre - neighbour
-            powered = jnp.exp(0.4 * jnp.log(differ * differ))
-            above = 1.0 + powered
-            coefficient = (weight_nb + (weight_nb * QRATIO) * powered) / (above * above)
-            numerator = numerator + coefficient * neighbour
-            denominator = denominator + coefficient
+            bend = jnp.tanh(0.2 * jnp.log(differ * differ))
+            coefficient = (1.0 - bend) * (4.0 - bend)
+            scaled = coefficient * neighbour
+            above[weight_nb] = above[weight_nb] + scaled if weight_nb in above else scaled
+            below[weight_nb] = below[weight_nb] + coefficient if weight_nb in below else coefficient
+        numerator = average
+        denominator = jnp.ones_like(average)
+        for weight_nb in above:
+            numerator = numerator + (0.1 * weight_nb) * above[weight_nb]
+            denominator = denominator + (0.1 * weight_nb) * below[weight_nb]
         out.append(numerator / denominator)
     return out
 
@@ -236,20 +284,19 @@
     share = measured.shape[2]
     f32 = jnp.float32
 
-    half = views // 2
     starts = offsets.reshape(1, views)
-    sent = pl.pallas_call(
+    sent, blocks = pl.pallas_call(
         project_kernel,
-        grid=(2,),
-        in_specs=[
-            SMEM,
-            pl.BlockSpec(states.shape, lambda i: (0, 0, 0, 0)),
-            pl.BlockSpec((half, 1, foot, pixels), lambda i: (i, 0, 0, 0)),
-            pl.BlockSpec((half, slices, share), lambda i: (i, 0, 0)),
-            pl.BlockSpec((half, slices, share), lambda i: (i, 0, 0)),
+        in_specs=[SMEM, ANY, ANY, ANY, ANY],
+        out_specs=[VMEM, VMEM],
+        out_shape=[near_shape(2 * n_tile, LANES), near_shape(*footprints.shape)],
+        scratch_shapes=[
+            pltpu.VMEM(states.shape, f32),
+            pltpu.VMEM(measured.shape, f32),
+            pltpu.VMEM(weights.shape, f32),
+            pltpu.SemaphoreType.DMA((PIECES,)),
+            pltpu.SemaphoreType.DMA((3,)),
         ],
-        out_specs=pl.BlockSpec((2 * n_tile, LANES), lambda i: (0, 0)),
-        out_shape=near_shape(2 * n_tile, LANES),
         name="project",
     )(starts, states, footprints, measured, weights)
     bands = lax.all_to_all(sent.reshape(n_tile, 2, LANES), "tile", 0, 0, tiled=True)
@@ -268,7 +315,7 @@
         out_specs=VMEM,
         out_shape=near_shape(slices, pixels),
         name="gradient",
-    )(starts, near(windows.reshape(n_tile, LANES)), states_near, near(footprints))
+    )(starts, near(windows.reshape(n_tile, LANES)), states_near, near(blocks))
     half = n_agent // 2
     both = lax.all_gather(reflect, "agent", axis=0, axis_index_groups=[[y, half + y] for y in range(half)])
     copies = pl.pallas_call(

time: 81.2 us -> 81.7 us (level)
    pallas_call x1, Pallas kernels: 1.82 us -> 2.75 us  [shards(): pl.pallas_call(project_kernel, in_specs=[SMEM, ANY, ANY, ANY, ANY], out_s...]
where the time goes in v4:
time: 81.7 us; the launch traced here: 81.2 us
  blocking collectives  70 us (86%)
  Pallas kernels  5.53 us (7%)
  starting transfers between devices  2.59 us (3%)
  waiting for transfers between devices  2.46 us (3%)
    all_to_all x1, blocking collectives, shards(): lax.all_to_all(sent.reshape(n_tile, 2, LANES), 'tile', 0, 0, tiled=True)  29.6 us
    all_to_all x1, blocking collectives, shards(): lax.all_to_all(back.reshape(n_tile, 1, LANES), 'tile', 0, 0, tiled=True)  17.1 us
    all_gather x1, blocking collectives, shards(): lax.all_gather(reflect, 'agent', axis=0, axis_index_groups=[[y, half + y]...  12 us
    all_to_all x1, blocking collectives, shards(): lax.all_to_all(copies, axes, 0, 0, tiled=True, axis_index_groups=chip_gro...  11.3 us
    pallas_call x1, Pallas kernels, shards(): pl.pallas_call(project_kernel, in_specs=[SMEM, ANY, ANY, ANY, ANY], out_s...  2.75 us
    ppermute x1, starting transfers between devices, shards(): side = lax.ppermute(mean, axes, side_pairs(n_tile, n_agent, 16))  2.59 us
    ppermute x1, waiting for transfers between devices, shards(): side = lax.ppermute(mean, axes, side_pairs(n_tile, n_agent, 16))  2.46 us
  transfers between devices with their start and end apart: 1, of which 1 were waited for; matrix products, arithmetic and copies ran while one was open for 0% of the time, Pallas kernels for 0%

profile of v4, /device:TPU:1, one launch (start us, length us, event | category | flops | bytes accessed | tf_op | source)
XLA Modules:
  0.0 81.2 jit_solution(14704794199105549431)
XLA Ops:
  0.6 2.8 %project.1 = (f32[128,128]{1,0:T(8,128)S(1)}, f32[8,1,64,512]{3,2,1,0:T(8,128)S(1)}) custom-call(s32[1,8]{1,0:T(1,128)} %bitcast.13, f32[1,8,2,256]{3,2,1,0:T(2,128)} %states_ref.3, f32[8,1,64,512]{3,2,1,0:T(8,128)} %blocks_hbm.1, f32[8,8,32]{2,1,0:T(8,128)} %measured_hbm.1, f32[8,8,32]{2,1,0:T(8,128)} %weights_hbm.1), custom_call_target="tpu_custom_call" | custom-call | tf_op jit(solution)/shard_map/project/pallas_call | solution.py:288
  3.4 29.6 %all_to_all.15 = f32[64,2,128]{2,1,0:T(2,128)S(1)} all-to-all(f32[64,2,128]{2,1,0:T(2,128)S(1)} %bitcast.12), channel_id=1, replica_groups=mesh['tile'=64,'agent'=8] {'tile'}, dimensions={0} | all-to-all | bytes 131072 | tf_op jit(solution)/shard_map/all_to_all | solution.py:302
  33.0 0.6 residual.1
  33.6 0.0 copy-start
  33.6 17.1 %all_to_all.16 = f32[64,1,128]{2,1,0:T(1,128)S(1)} all-to-all(f32[64,1,128]{2,1,0:T(1,128)S(1)} %bitcast.10), channel_id=1, replica_groups=mesh['tile'=64,'agent'=8] {'tile'}, dimensions={0} | all-to-all | bytes 65536 | tf_op jit(solution)/shard_map/all_to_all | solution.py:310
  50.7 0.0 copy-done
  50.7 1.0 %gradient.1.reflect_ref = f32[8,512]{1,0:T(8,128)S(1)} custom-call(s32[1,8]{1,0:T(1,128)} %bitcast.14, f32[64,128]{1,0:T(8,128)S(1)} %bitcast.9, f32[1,8,2,256]{3,2,1,0:T(2,128)S(1)} %copy-done, f32[8,1,64,512]{3,2,1,0:T(8,128)S(1)} %get-tuple-element.7.blocks_ref), custom_call_target="tpu_custom_call" | custom-call | tf_op jit(solution)/shard_map/gradient/pallas_call | solution.py:312
  51.7 12.0 %all-gather = f32[16,512]{1,0:T(8,128)S(1)} all-gather(f32[8,512]{1,0:T(8,128)S(1)} %gradient.1.reflect_ref), channel_id=2, replica_groups={{0,4},{1,5},{2,6},{3,7},{8,12},{9,13},{10,14},{11,15},{16,20},{17,21},{..., dimensions={0}, use_global_device_ids=true | all-gather | bytes 49152 | tf_op jit(solution)/shard_map/all_gather | solution.py:320
  63.7 11.3 %all_to_all.17.in_ref = f32[8,8,512]{2,1,0:T(8,128)S(1)} all-to-all(f32[8,8,512]{2,1,0:T(8,128)S(1)} %pair.1), channel_id=1, replica_groups={{0,1,2,3,8,9,10,11},{4,5,6,7,12,13,14,15},{16,17,18,19,24,25,26,27},{20..., dimensions={0} | all-to-all | bytes 262144 | tf_op jit(solution)/shard_map/all_to_all | solution.py:329
  75.0 2.6 %collective-permute-start = (f32[8,512]{1,0:T(8,128)S(1)}, f32[8,512]{1,0:T(8,128)S(1)}, u32[]{:S(2)}, u32[]{:S(2)}) collective-permute-start(f32[8,512]{1,0:T(8,128)S(1)} %get-tuple-element.8.mean_ref), channel_id=1, source_target_pairs={{8,16},{16,8},{9,17},{17,9},{10,18},{18,10},{11,19},{19,11},{12,20... | collective-permute-start | bytes 49160 | tf_op jit(solution)/shard_map/ppermute | solution.py:337
  77.5 2.5 %collective-permute-done.side_ref = f32[8,512]{1,0:T(8,128)S(1)} collective-permute-done((f32[8,512]{1,0:T(8,128)S(1)}, f32[8,512]{1,0:T(8,128)S(1)}, u32[]{:S(2)}, u32[]{:S(2)}) %collective-permute-start) | collective-permute-done | bytes 16416 | tf_op jit(solution)/shard_map/ppermute | solution.py:337
  80.0 1.2 %prior.1 = (f32[1,8,2,256]{3,2,1,0:T(2,128)}, f32[8,2,256]{2,1,0:T(2,128)}) custom-call(f32[8,512]{1,0:T(8,128)S(1)} %get-tuple-element.8.mean_ref, f32[8,512]{1,0:T(8,128)S(1)} %get-tuple-element.9.near_ref, f32[8,512]{1,0:T(8,128)S(1)} %collective-permute-done.side_ref, f32[1,8,2,256]{3,2,1,0:T(2,128)S(1)} %copy-done, f32[8,512]{1,0:T(8,128)S(1)} %gradient.1.reflect_ref), custom_call_target="tpu_custom_call" | custom-call | tf_op jit(solution)/shard_map/prior/pallas_call | solution.py:338
  (2 shorter events, 0.0 us)
Async XLA Ops:
  33.6 17.1 %copy-start = (f32[1,8,2,256]{3,2,1,0:T(2,128)S(1)}, f32[1,8,2,256]{3,2,1,0:T(2,128)}, u32[]{:S(2)}) copy-start(f32[1,8,2,256]{3,2,1,0:T(2,128)} %states_ref.3) | copy-start | bytes 49156
  75.0 5.1 %collective-permute-start = (f32[8,512]{1,0:T(8,128)S(1)}, f32[8,512]{1,0:T(8,128)S(1)}, u32[]{:S(2)}, u32[]{:S(2)}) collective-permute-start(f32[8,512]{1,0:T(8,128)S(1)} %get-tuple-element.8.mean_ref), channel_id=1, source_target_pairs={{8,16},{16,8},{9,17},{17,9},{10,18},{18,10},{11,19},{19,11},{12,20... | collective-permute-start | bytes 49160 | tf_op jit(solution)/shard_map/ppermute | solution.py:337

commit v5 on v3

--- a/solution.py
+++ b/solution.py
@@ -8,7 +8,6 @@
 SWEEPS = 2
 STEP_SIZE = 0.25
 RELAX = 0.6
-QRATIO = 0.6
 BLOCK = 32
 LANES = 128
 
@@ -83,6 +82,20 @@
         out_ref[pl.ds(start + 1, slices, stride=2), :] = second
 
 
+def thirds(x):
+    high = x.astype(jnp.bfloat16)
+    rest = x - high.astype(jnp.float32)
+    mid = rest.astype(jnp.bfloat16)
+    low = (rest - mid.astype(jnp.float32)).astype(jnp.bfloat16)
+    return jnp.concatenate([high, mid, low], axis=1)
+
+
+def select_dot(onehot, x, dims):
+    width = x.shape[1]
+    all_three = lax.dot_general(onehot, thirds(x), (dims, ((), ())), preferred_element_type=jnp.float32)
+    return all_three[:, :width] + (all_three[:, width : 2 * width] + all_three[:, 2 * width :])
+
+
 def residual_kernel(in_ref, out_ref):
     tiles = out_ref.shape[0]
     share = BLOCK
@@ -90,10 +103,8 @@
     first = in_ref[pl.ds(0, tiles, stride=2), :]
     second = in_ref[pl.ds(1, tiles, stride=2), :]
     base = second[:, share : share + 1].astype(jnp.int32)
-    onehot = jnp.where(lane_iota((tiles, tiles)) == base, 1.0, 0.0)
-    placed = lax.dot_general(
-        onehot, first, (((0,), (0,)), ((), ())), precision=lax.Precision.HIGHEST, preferred_element_type=jnp.float32
-    )
+    onehot = jnp.where(lane_iota((tiles, tiles)) == base, 1.0, 0.0).astype(jnp.bfloat16)
+    placed = select_dot(onehot, first, ((0,), (0,)))
     total = placed
     for part in (1, 2):
         moved = pltpu.roll(placed, part, 0)
@@ -104,7 +115,7 @@
     for part in (1, 2):
         moved = pltpu.roll(residual, tiles - part, 0)
         windows += pltpu.roll(moved, part * share, 1)
-    out_ref[...] = jnp.dot(onehot, windows, precision=lax.Precision.HIGHEST, preferred_element_type=jnp.float32)
+    out_ref[...] = select_dot(onehot, windows, ((1,), (0,)))
 
 
 def gradient_kernel(offsets_ref, windows_ref, states_ref, blocks_ref, out_ref):
@@ -137,7 +148,7 @@
         out_ref[copy] = total
 
 
-def mean_kernel(in_ref, own_ref, other_ref):
+def mean_kernel(in_ref, own_ref, side_ref):
     count = in_ref.shape[0] // 2
     means = []
     for half in range(2):
@@ -146,8 +157,8 @@
             total = total + in_ref[half * count + member]
         means.append(total * (0.5 / count))
     odd = lax.axis_index("tile") % 2 == 1
-    own_ref[...] = jnp.where(odd, means[1], means[0])
-    other_ref[...] = jnp.where(odd, means[0], means[1])
+    own_ref[...] = jnp.where(odd, means[0], means[1])
+    side_ref[...] = jnp.where(odd, means[1], means[0])
 
 
 def shifted(row, a, c):
@@ -169,30 +180,34 @@
     out = []
     for index, average in enumerate(averages):
         centre = rows[index + 1]
-        numerator = average
-        denominator = jnp.ones_like(average)
+        above, below = {}, {}
         for a, b, c, weight_nb in table:
             neighbour = moved[index + 1 + b][(a, c)]
             differ = centre - neighbour
-            powered = jnp.exp(0.4 * jnp.log(differ * differ))
-            above = 1.0 + powered
-            coefficient = (weight_nb + (weight_nb * QRATIO) * powered) / (above * above)
-            numerator = numerator + coefficient * neighbour
-            denominator = denominator + coefficient
+            bend = jnp.tanh(0.2 * jnp.log(differ * differ))
+            coefficient = (1.0 - bend) * (4.0 - bend)
+            scaled = coefficient * neighbour
+            above[weight_nb] = above[weight_nb] + scaled if weight_nb in above else scaled
+            below[weight_nb] = below[weight_nb] + coefficient if weight_nb in below else coefficient
+        numerator = average
+        denominator = jnp.ones_like(average)
+        for weight_nb in above:
+            numerator = numerator + (0.1 * weight_nb) * above[weight_nb]
+            denominator = denominator + (0.1 * weight_nb) * below[weight_nb]
         out.append(numerator / denominator)
     return out
 
 
-def prior_kernel(mean_ref, near_ref, side_ref, states_ref, reflect_ref, new_ref, prior_ref):
+def prior_kernel(chip_ref, side_ref, states_ref, reflect_ref, new_ref, prior_ref):
     width = states_ref.shape[3]
     tile = lax.axis_index("tile")
     last = lax.axis_size("tile") - 1
     odd = tile % 2 == 1
-    near = near_ref[...]
     side = side_ref[...]
-    mean = mean_ref[...]
-    above = jnp.where(odd, near, side)
-    below = jnp.where(odd, side, near)
+    even, other = chip_ref[0], chip_ref[1]
+    above = jnp.where(odd, even, side)
+    mean = jnp.where(odd, other, even)
+    below = jnp.where(odd, side, other)
     above = jnp.where(tile == 0, 0.0, above)
     below = jnp.where(tile == last, 0.0, below)
     rows = [x[:, i * width : (i + 1) * width] for x in (above, mean, below) for i in range(2)]
@@ -207,25 +222,17 @@
         new_ref[0, :, row, :] = (1.0 - RELAX) * states_ref[0, :, row, :] + RELAX * (2.0 * final[row] - reflect)
 
 
-def side_pairs(n_tile, n_agent, per_x):
-    pairs = []
-    for tile in range(1, n_tile - 1, 2):
-        other = tile + 1
-        for agent in range(n_agent):
-            crossing = tile // per_x != other // per_x
-            partner = (agent + n_agent // 2) % n_agent if crossing else agent
-            one, two = tile * n_agent + agent, other * n_agent + partner
-            pairs += [(one, two), (two, one)]
-    return pairs
-
-
-def chip_groups(n_tile, n_agent):
+def facing_groups(n_tile, n_agent, per_x):
     half = n_agent // 2
-    return [
-        [(tile + core) * n_agent + first + y for core in range(2) for y in range(half)]
-        for tile in range(0, n_tile, 2)
-        for first in (0, half)
-    ]
+    groups = []
+    for odd in range(1, n_tile, 2):
+        even = (odd + 1) % n_tile
+        for first in (0, half):
+            second = first if odd // per_x == even // per_x else half - first
+            groups.append(
+                [odd * n_agent + first + y for y in range(half)] + [even * n_agent + second + y for y in range(half)]
+            )
+    return groups
 
 
 def shards(states, footprints, offsets, measured, weights):
@@ -279,25 +286,25 @@
         name="pair",
     )(near(both))
     axes = ("tile", "agent")
-    shares = lax.all_to_all(copies, axes, 0, 0, tiled=True, axis_index_groups=chip_groups(n_tile, n_agent))
-    mean, core = pl.pallas_call(
+    shares = lax.all_to_all(copies, axes, 0, 0, tiled=True, axis_index_groups=facing_groups(n_tile, n_agent, 16))
+    mean, side = pl.pallas_call(
         mean_kernel,
         in_specs=[VMEM],
         out_specs=[VMEM, VMEM],
         out_shape=[near_shape(slices, pixels), near_shape(slices, pixels)],
         name="mean",
     )(near(shares))
-    side = lax.ppermute(mean, axes, side_pairs(n_tile, n_agent, 16))
+    chip = lax.all_gather(mean, "tile", axis=0, axis_index_groups=[[t, t + 1] for t in range(0, n_tile, 2)])
     new_states, prior = pl.pallas_call(
         prior_kernel,
-        in_specs=[VMEM] * 5,
+        in_specs=[VMEM] * 4,
         out_specs=[VMEM, VMEM],
         out_shape=[
             jax.ShapeDtypeStruct(states.shape, f32),
             jax.ShapeDtypeStruct((slices, height, width), f32),
         ],
         name="prior",
-    )(near(mean), near(core), near(side), states_near, near(reflect))
+    )(near(chip), near(side), states_near, near(reflect))
     return new_states, prior
 
 

time: 81.2 us -> 81.2 us (level)
  blocking collectives: 70.1 us -> 75.7 us
  starting transfers between devices: 2.59 us -> 0 us
  waiting for transfers between devices: 2.46 us -> 0 us
    all_gather x0 -> x1, blocking collectives: none -> 5.03 us  [shards(): lax.all_gather(mean, 'tile', axis=0, axis_index_groups=[[t, t + 1] for t...]
    ppermute x1 -> x0, starting transfers between devices: 2.59 us -> none  [shards(): side = lax.ppermute(mean, axes, side_pairs(n_tile, n_agent, 16))]
    ppermute x1 -> x0, waiting for transfers between devices: 2.46 us -> none  [shards(): side = lax.ppermute(mean, axes, side_pairs(n_tile, n_agent, 16))]
  transfers between devices with their start and end apart: 1 -> 0, of which waited for: 1 -> 0; matrix products, arithmetic and copies ran while one was open for 0% -> 0% of each run, Pallas kernels for 0% -> 0%
where the time goes in v5:
time: 81.2 us; the launch traced here: 80.9 us
  blocking collectives  75.7 us (93%)
  Pallas kernels  4.59 us (6%)
    all_to_all x1, blocking collectives, shards(): lax.all_to_all(sent.reshape(n_tile, 2, LANES), 'tile', 0, 0, tiled=True)  29.6 us
    all_to_all x1, blocking collectives, shards(): lax.all_to_all(back.reshape(n_tile, 1, LANES), 'tile', 0, 0, tiled=True)  17.1 us
    all_gather x1, blocking collectives, shards(): lax.all_gather(reflect, 'agent', axis=0, axis_index_groups=[[y, half + y]...  12 us
    all_to_all x1, blocking collectives, shards(): lax.all_to_all(copies, axes, 0, 0, tiled=True, axis_index_groups=facing_g...  11.9 us
    all_gather x1, blocking collectives, shards(): lax.all_gather(mean, 'tile', axis=0, axis_index_groups=[[t, t + 1] for t...  5.03 us
    pallas_call x1, Pallas kernels, shards(): pl.pallas_call(project_kernel, grid=(2,), in_specs=[SMEM, pl.BlockSpec(st...  1.82 us

profile of v5, /device:TPU:1, one launch (start us, length us, event | category | flops | bytes accessed | tf_op | source)
XLA Modules:
  0.0 80.9 jit_solution(11406981726531243694)
XLA Ops:
  0.6 0.0 copy-start
  0.6 1.8 %project.1 = f32[128,128]{1,0:T(8,128)S(1)} custom-call(s32[1,8]{1,0:T(1,128)} %bitcast.15, f32[1,8,2,256]{3,2,1,0:T(2,128)} %states_ref.5, f32[8,1,64,512]{3,2,1,0:T(8,128)} %blocks_ref.3, f32[8,8,32]{2,1,0:T(8,128)} %measured_ref.1, f32[8,8,32]{2,1,0:T(8,128)} %weights_ref.1), custom_call_target="tpu_custom_call" | custom-call | tf_op jit(solution)/shard_map/project/pallas_call | solution.py:248
  2.5 29.6 %all_to_all.15 = f32[64,2,128]{2,1,0:T(2,128)S(1)} all-to-all(f32[64,2,128]{2,1,0:T(2,128)S(1)} %bitcast.9), channel_id=1, replica_groups=mesh['tile'=64,'agent'=8] {'tile'}, dimensions={0} | all-to-all | bytes 131072 | tf_op jit(solution)/shard_map/all_to_all | solution.py:262
  32.1 0.6 residual.1
  32.7 0.0 copy-start.1
  32.7 17.1 %all_to_all.16 = f32[64,1,128]{2,1,0:T(1,128)S(1)} all-to-all(f32[64,1,128]{2,1,0:T(1,128)S(1)} %bitcast.11), channel_id=1, replica_groups=mesh['tile'=64,'agent'=8] {'tile'}, dimensions={0} | all-to-all | bytes 65536 | tf_op jit(solution)/shard_map/all_to_all | solution.py:270
  49.8 0.0 copy-done
  49.8 0.0 copy-done.1
  49.8 1.0 %gradient.1.reflect_ref = f32[8,512]{1,0:T(8,128)S(1)} custom-call(s32[1,8]{1,0:T(1,128)} %bitcast.16, f32[64,128]{1,0:T(8,128)S(1)} %bitcast.12, f32[1,8,2,256]{3,2,1,0:T(2,128)S(1)} %copy-done.1, f32[8,1,64,512]{3,2,1,0:T(8,128)S(1)} %copy-done), custom_call_target="tpu_custom_call" | custom-call | tf_op jit(solution)/shard_map/gradient/pallas_call | solution.py:272
  50.8 12.0 %all-gather = f32[16,512]{1,0:T(8,128)S(1)} all-gather(f32[8,512]{1,0:T(8,128)S(1)} %gradient.1.reflect_ref), channel_id=2, replica_groups={{0,4},{1,5},{2,6},{3,7},{8,12},{9,13},{10,14},{11,15},{16,20},{17,21},{..., dimensions={0}, use_global_device_ids=true | all-gather | bytes 49152 | tf_op jit(solution)/shard_map/all_gather | solution.py:280
  62.8 11.9 %all_to_all.17.in_ref = f32[8,8,512]{2,1,0:T(8,128)S(1)} all-to-all(f32[8,8,512]{2,1,0:T(8,128)S(1)} %pair.1), channel_id=1, replica_groups={{8,9,10,11,16,17,18,19},{12,13,14,15,20,21,22,23},{24,25,26,27,32,33,34..., dimensions={0} | all-to-all | bytes 262144 | tf_op jit(solution)/shard_map/all_to_all | solution.py:289
  74.7 5.0 %all-gather.1 = f32[16,512]{1,0:T(8,128)S(1)} all-gather(f32[8,512]{1,0:T(8,128)S(1)} %get-tuple-element.4), channel_id=3, replica_groups={{0,8},{16,24},{32,40},{48,56},{64,72},{80,88},{96,104},{112,120},{128,1..., dimensions={0}, use_global_device_ids=true | all-gather | bytes 49152 | tf_op jit(solution)/shard_map/all_gather | solution.py:297
  79.7 1.2 %prior.1 = (f32[1,8,2,256]{3,2,1,0:T(2,128)}, f32[8,2,256]{2,1,0:T(2,128)}) custom-call(f32[2,8,512]{2,1,0:T(8,128)S(1)} %bitcast.14, f32[8,512]{1,0:T(8,128)S(1)} %get-tuple-element.5.side_ref, f32[1,8,2,256]{3,2,1,0:T(2,128)S(1)} %copy-done.1, f32[8,512]{1,0:T(8,128)S(1)} %gradient.1.reflect_ref), custom_call_target="tpu_custom_call" | custom-call | tf_op jit(solution)/shard_map/prior/pallas_call | solution.py:298
  (2 shorter events, 0.0 us)
Async XLA Ops:
  0.6 49.1 %copy-start = (f32[8,1,64,512]{3,2,1,0:T(8,128)S(1)}, f32[8,1,64,512]{3,2,1,0:T(8,128)}, u32[]{:S(2)}) copy-start(f32[8,1,64,512]{3,2,1,0:T(8,128)} %blocks_ref.3) | copy-start | bytes 3145732
  32.7 17.1 %copy-start.1 = (f32[1,8,2,256]{3,2,1,0:T(2,128)S(1)}, f32[1,8,2,256]{3,2,1,0:T(2,128)}, u32[]{:S(2)}) copy-start(f32[1,8,2,256]{3,2,1,0:T(2,128)} %states_ref.5) | copy-start | bytes 49156

commit v6 on v5

--- a/solution.py
+++ b/solution.py
@@ -142,23 +142,14 @@
         out_ref[:, at] = states_ref[0, :, row, :] - (2.0 * STEP_SIZE) * gradient[:, at]
 
 
-def pair_kernel(in_ref, out_ref):
-    total = in_ref[0] + in_ref[1]
+def sum_kernel(in_ref, out_ref):
+    out_ref[...] = in_ref[0] + in_ref[1]
+
+
+def copy_kernel(in_ref, out_ref):
+    both = in_ref[...]
     for copy in range(out_ref.shape[0]):
-        out_ref[copy] = total
-
-
-def mean_kernel(in_ref, own_ref, side_ref):
-    count = in_ref.shape[0] // 2
-    means = []
-    for half in range(2):
-        total = in_ref[half * count]
-        for member in range(1, count):
-            total = total + in_ref[half * count + member]
-        means.append(total * (0.5 / count))
-    odd = lax.axis_index("tile") % 2 == 1
-    own_ref[...] = jnp.where(odd, means[0], means[1])
-    side_ref[...] = jnp.where(odd, means[1], means[0])
+        out_ref[copy] = both
 
 
 def shifted(row, a, c):
@@ -198,16 +189,21 @@
     return out
 
 
-def prior_kernel(chip_ref, side_ref, states_ref, reflect_ref, new_ref, prior_ref):
+def prior_kernel(shares_ref, states_ref, reflect_ref, new_ref, prior_ref):
     width = states_ref.shape[3]
     tile = lax.axis_index("tile")
     last = lax.axis_size("tile") - 1
     odd = tile % 2 == 1
-    side = side_ref[...]
-    even, other = chip_ref[0], chip_ref[1]
-    above = jnp.where(odd, even, side)
-    mean = jnp.where(odd, other, even)
-    below = jnp.where(odd, side, other)
+    count = shares_ref.shape[0] // 2
+
+    def mean_of(chip, core):
+        total = shares_ref[chip * count, core]
+        for member in range(1, count):
+            total = total + shares_ref[chip * count + member, core]
+        return total * (0.5 / count)
+
+    four = [mean_of(chip, core) for chip in range(2) for core in range(2)]
+    above, mean, below = [jnp.where(odd, four[i], four[i + 1]) for i in range(3)]
     above = jnp.where(tile == 0, 0.0, above)
     below = jnp.where(tile == last, 0.0, below)
     rows = [x[:, i * width : (i + 1) * width] for x in (above, mean, below) for i in range(2)]
@@ -278,33 +274,33 @@
     )(starts, near(windows.reshape(n_tile, LANES)), states_near, near(footprints))
     half = n_agent // 2
     both = lax.all_gather(reflect, "agent", axis=0, axis_index_groups=[[y, half + y] for y in range(half)])
-    copies = pl.pallas_call(
-        pair_kernel,
+    summed = pl.pallas_call(
+        sum_kernel,
         in_specs=[VMEM],
         out_specs=VMEM,
-        out_shape=near_shape(n_agent, slices, pixels),
-        name="pair",
+        out_shape=near_shape(slices, pixels),
+        name="sum",
     )(near(both))
+    chip = lax.all_gather(summed, "tile", axis=0, axis_index_groups=[[t, t + 1] for t in range(0, n_tile, 2)])
+    copies = pl.pallas_call(
+        copy_kernel,
+        in_specs=[VMEM],
+        out_specs=VMEM,
+        out_shape=near_shape(n_agent, 2, slices, pixels),
+        name="copies",
+    )(near(chip))
     axes = ("tile", "agent")
     shares = lax.all_to_all(copies, axes, 0, 0, tiled=True, axis_index_groups=facing_groups(n_tile, n_agent, 16))
-    mean, side = pl.pallas_call(
-        mean_kernel,
-        in_specs=[VMEM],
-        out_specs=[VMEM, VMEM],
-        out_shape=[near_shape(slices, pixels), near_shape(slices, pixels)],
-        name="mean",
-    )(near(shares))
-    chip = lax.all_gather(mean, "tile", axis=0, axis_index_groups=[[t, t + 1] for t in range(0, n_tile, 2)])
     new_states, prior = pl.pallas_call(
         prior_kernel,
-        in_specs=[VMEM] * 4,
+        in_specs=[VMEM] * 3,
         out_specs=[VMEM, VMEM],
         out_shape=[
             jax.ShapeDtypeStruct(states.shape, f32),
             jax.ShapeDtypeStruct((slices, height, width), f32),
         ],
         name="prior",
-    )(near(chip), near(side), states_near, near(reflect))
+    )(near(shares), states_near, near(reflect))
     return new_states, prior
 
 

time: 81.2 us -> 79.7 us (0.982); the launches traced: 80.9 us -> 78.2 us
  blocking collectives: 75.7 us -> 73 us
    all_gather x1, blocking collectives: 5.03 us -> 3.27 us  [shards(): lax.all_gather(summed, 'tile', axis=0, axis_index_groups=[[t, t + 1] for...]
    all_to_all x1, blocking collectives: 11.9 us -> 11 us  [shards(): lax.all_to_all(copies, axes, 0, 0, tiled=True, axis_index_groups=facing_g...]
where the time goes in v6:
time: 79.7 us; the launch traced here: 78.2 us
  blocking collectives  73 us (92%)
  Pallas kernels  4.59 us (6%)
    all_to_all x1, blocking collectives, shards(): lax.all_to_all(sent.reshape(n_tile, 2, LANES), 'tile', 0, 0, tiled=True)  29.6 us
    all_to_all x1, blocking collectives, shards(): lax.all_to_all(back.reshape(n_tile, 1, LANES), 'tile', 0, 0, tiled=True)  17.1 us
    all_gather x1, blocking collectives, shards(): lax.all_gather(reflect, 'agent', axis=0, axis_index_groups=[[y, half + y]...  12 us
    all_to_all x1, blocking collectives, shards(): lax.all_to_all(copies, axes, 0, 0, tiled=True, axis_index_groups=facing_g...  11 us
    all_gather x1, blocking collectives, shards(): lax.all_gather(summed, 'tile', axis=0, axis_index_groups=[[t, t + 1] for...  3.27 us
    pallas_call x1, Pallas kernels, shards(): pl.pallas_call(project_kernel, grid=(2,), in_specs=[SMEM, pl.BlockSpec(st...  1.82 us

profile of v6, /device:TPU:1, one launch (start us, length us, event | category | flops | bytes accessed | tf_op | source)
XLA Modules:
  0.0 78.2 jit_solution(13772953422845019081)
XLA Ops:
  0.6 0.0 copy-start
  0.6 1.8 %project.1 = f32[128,128]{1,0:T(8,128)S(1)} custom-call(s32[1,8]{1,0:T(1,128)} %bitcast.15, f32[1,8,2,256]{3,2,1,0:T(2,128)} %states_ref.5, f32[8,1,64,512]{3,2,1,0:T(8,128)} %blocks_ref.3, f32[8,8,32]{2,1,0:T(8,128)} %measured_ref.1, f32[8,8,32]{2,1,0:T(8,128)} %weights_ref.1), custom_call_target="tpu_custom_call" | custom-call | tf_op jit(solution)/shard_map/project/pallas_call | solution.py:244
  2.5 29.6 %all_to_all.15 = f32[64,2,128]{2,1,0:T(2,128)S(1)} all-to-all(f32[64,2,128]{2,1,0:T(2,128)S(1)} %bitcast.9), channel_id=1, replica_groups=mesh['tile'=64,'agent'=8] {'tile'}, dimensions={0} | all-to-all | bytes 131072 | tf_op jit(solution)/shard_map/all_to_all | solution.py:258
  32.1 0.6 residual.1
  32.7 0.0 copy-start.1
  32.7 17.1 %all_to_all.16 = f32[64,1,128]{2,1,0:T(1,128)S(1)} all-to-all(f32[64,1,128]{2,1,0:T(1,128)S(1)} %bitcast.11), channel_id=1, replica_groups=mesh['tile'=64,'agent'=8] {'tile'}, dimensions={0} | all-to-all | bytes 65536 | tf_op jit(solution)/shard_map/all_to_all | solution.py:266
  49.8 0.0 copy-done
  49.8 0.0 copy-done.1
  49.8 1.0 %gradient.1.reflect_ref = f32[8,512]{1,0:T(8,128)S(1)} custom-call(s32[1,8]{1,0:T(1,128)} %bitcast.16, f32[64,128]{1,0:T(8,128)S(1)} %bitcast.12, f32[1,8,2,256]{3,2,1,0:T(2,128)S(1)} %copy-done.1, f32[8,1,64,512]{3,2,1,0:T(8,128)S(1)} %copy-done), custom_call_target="tpu_custom_call" | custom-call | tf_op jit(solution)/shard_map/gradient/pallas_call | solution.py:268
  50.8 12.0 %all-gather = f32[16,512]{1,0:T(8,128)S(1)} all-gather(f32[8,512]{1,0:T(8,128)S(1)} %gradient.1.reflect_ref), channel_id=2, replica_groups={{0,4},{1,5},{2,6},{3,7},{8,12},{9,13},{10,14},{11,15},{16,20},{17,21},{..., dimensions={0}, use_global_device_ids=true | all-gather | bytes 49152 | tf_op jit(solution)/shard_map/all_gather | solution.py:276
  62.7 3.3 %all-gather.1 = f32[16,512]{1,0:T(8,128)S(1)} all-gather(f32[8,512]{1,0:T(8,128)S(1)} %sum.1), channel_id=3, replica_groups={{0,8},{16,24},{32,40},{48,56},{64,72},{80,88},{96,104},{112,120},{128,1..., dimensions={0}, use_global_device_ids=true | all-gather | bytes 49152 | tf_op jit(solution)/shard_map/all_gather | solution.py:284
  66.0 11.0 %all_to_all.17.shares_ref = f32[8,2,8,512]{3,2,1,0:T(8,128)S(1)} all-to-all(f32[8,2,8,512]{3,2,1,0:T(8,128)S(1)} %copies.1), channel_id=1, replica_groups={{8,9,10,11,16,17,18,19},{12,13,14,15,20,21,22,23},{24,25,26,27,32,33,34..., dimensions={0} | all-to-all | bytes 524288 | tf_op jit(solution)/shard_map/all_to_all | solution.py:293
  77.0 1.2 %prior.1 = (f32[1,8,2,256]{3,2,1,0:T(2,128)}, f32[8,2,256]{2,1,0:T(2,128)}) custom-call(f32[8,2,8,512]{3,2,1,0:T(8,128)S(1)} %all_to_all.17.shares_ref, f32[1,8,2,256]{3,2,1,0:T(2,128)S(1)} %copy-done.1, f32[8,512]{1,0:T(8,128)S(1)} %gradient.1.reflect_ref), custom_call_target="tpu_custom_call" | custom-call | tf_op jit(solution)/shard_map/prior/pallas_call | solution.py:294
  (2 shorter events, 0.0 us)
Async XLA Ops:
  0.6 49.1 %copy-start = (f32[8,1,64,512]{3,2,1,0:T(8,128)S(1)}, f32[8,1,64,512]{3,2,1,0:T(8,128)}, u32[]{:S(2)}) copy-start(f32[8,1,64,512]{3,2,1,0:T(8,128)} %blocks_ref.3) | copy-start | bytes 3145732
  32.7 17.1 %copy-start.1 = (f32[1,8,2,256]{3,2,1,0:T(2,128)S(1)}, f32[1,8,2,256]{3,2,1,0:T(2,128)}, u32[]{:S(2)}) copy-start(f32[1,8,2,256]{3,2,1,0:T(2,128)} %states_ref.5) | copy-start | bytes 49156

commit v7 on v6

--- a/solution.py
+++ b/solution.py
@@ -10,6 +10,8 @@
 RELAX = 0.6
 BLOCK = 32
 LANES = 128
+MIDDLE = 40
+MIDDLE_FIRST = (2, 1, 3, 0)
 
 SMEM = pl.BlockSpec(memory_space=pltpu.SMEM)
 VMEM = pl.BlockSpec(memory_space=pltpu.VMEM)
@@ -96,6 +98,17 @@
     return all_three[:, :width] + (all_three[:, width : 2 * width] + all_three[:, 2 * width :])
 
 
+def tile_order(x):
+    row = lax.broadcasted_iota(jnp.int32, x.shape, 0)
+    return jnp.where(row == 0, x[MIDDLE : MIDDLE + 1], jnp.where(row == MIDDLE, x[0:1], x))
+
+
+def group_order(n_tile):
+    order = list(range(n_tile))
+    order[0], order[MIDDLE] = MIDDLE, 0
+    return order
+
+
 def residual_kernel(in_ref, out_ref):
     tiles = out_ref.shape[0]
     share = BLOCK
@@ -109,8 +122,8 @@
     for part in (1, 2):
         moved = pltpu.roll(placed, part, 0)
         total += pltpu.roll(moved, LANES - part * share, 1)
-    measured = pltpu.roll(first, share, 1)
-    residual = jnp.where(lane < share, second * (total - measured), 0.0)
+    measured = pltpu.roll(tile_order(first), share, 1)
+    residual = jnp.where(lane < share, tile_order(second) * (total - measured), 0.0)
     windows = residual
     for part in (1, 2):
         moved = pltpu.roll(residual, tiles - part, 0)
@@ -226,7 +239,7 @@
         for first in (0, half):
             second = first if odd // per_x == even // per_x else half - first
             groups.append(
-                [odd * n_agent + first + y for y in range(half)] + [even * n_agent + second + y for y in range(half)]
+                [odd * n_agent + first + y for y in MIDDLE_FIRST] + [even * n_agent + second + y for y in MIDDLE_FIRST]
             )
     return groups
 
@@ -255,7 +268,8 @@
         out_shape=near_shape(2 * n_tile, LANES),
         name="project",
     )(starts, states, footprints, measured, weights)
-    bands = lax.all_to_all(sent.reshape(n_tile, 2, LANES), "tile", 0, 0, tiled=True)
+    order = [group_order(n_tile)]
+    bands = lax.all_to_all(sent.reshape(n_tile, 2, LANES), "tile", 0, 0, tiled=True, axis_index_groups=order)
     back = pl.pallas_call(
         residual_kernel,
         in_specs=[VMEM],
@@ -263,7 +277,7 @@
         out_shape=near_shape(n_tile, LANES),
         name="residual",
     )(near(bands.reshape(2 * n_tile, LANES)))
-    windows = lax.all_to_all(back.reshape(n_tile, 1, LANES), "tile", 0, 0, tiled=True)
+    windows = lax.all_to_all(back.reshape(n_tile, 1, LANES), "tile", 0, 0, tiled=True, axis_index_groups=order)
     states_near = near(states)
     reflect = pl.pallas_call(
         gradient_kernel,

time: 79.7 us -> 72.8 us (0.913)
  the two profiles are of different devices: /device:TPU:1 before, /device:TPU:16 now
where the time goes in v7:
time: 72.8 us; the launch traced here: 72.5 us
  blocking collectives  67.3 us (92%)
  Pallas kernels  4.59 us (6%)
    all_to_all x1, blocking collectives, shards(): lax.all_to_all(sent.reshape(n_tile, 2, LANES), 'tile', 0, 0, tiled=True,...  22.1 us
    all_to_all x1, blocking collectives, shards(): lax.all_to_all(back.reshape(n_tile, 1, LANES), 'tile', 0, 0, tiled=True,...  15.2 us
    all_to_all x1, blocking collectives, shards(): lax.all_to_all(copies, axes, 0, 0, tiled=True, axis_index_groups=facing_g...  15.1 us
    all_gather x1, blocking collectives, shards(): lax.all_gather(reflect, 'agent', axis=0, axis_index_groups=[[y, half + y]...  13.1 us
    pallas_call x1, Pallas kernels, shards(): pl.pallas_call(project_kernel, grid=(2,), in_specs=[SMEM, pl.BlockSpec(st...  1.82 us
    all_gather x1, blocking collectives, shards(): lax.all_gather(summed, 'tile', axis=0, axis_index_groups=[[t, t + 1] for...  1.82 us

profile of v7, /device:TPU:16, one launch (start us, length us, event | category | flops | bytes accessed | tf_op | source)
XLA Modules:
  0.0 72.5 jit_solution(16760093911153299159)
XLA Ops:
  0.6 0.0 copy-start
  0.6 1.8 %project.1 = f32[128,128]{1,0:T(8,128)S(1)} custom-call(s32[1,8]{1,0:T(1,128)} %bitcast.15, f32[1,8,2,256]{3,2,1,0:T(2,128)} %states_ref.5, f32[8,1,64,512]{3,2,1,0:T(8,128)} %blocks_ref.3, f32[8,8,32]{2,1,0:T(8,128)} %measured_ref.1, f32[8,8,32]{2,1,0:T(8,128)} %weights_ref.1), custom_call_target="tpu_custom_call" | custom-call | tf_op jit(solution)/shard_map/project/pallas_call | solution.py:257
  2.5 22.1 %all_to_all.15 = f32[64,2,128]{2,1,0:T(2,128)S(1)} all-to-all(f32[64,2,128]{2,1,0:T(2,128)S(1)} %bitcast.9), channel_id=1, replica_groups={{320,8,16,24,32,40,48,56,64,72,80,88,96,104,112,120,128,136,144,152,160..., dimensions={0} | all-to-all | bytes 131072 | tf_op jit(solution)/shard_map/all_to_all | solution.py:272
  24.6 0.6 residual.1
  25.1 0.0 copy-start.1
  25.1 15.2 %all_to_all.16 = f32[64,1,128]{2,1,0:T(1,128)S(1)} all-to-all(f32[64,1,128]{2,1,0:T(1,128)S(1)} %bitcast.11), channel_id=1, replica_groups={{320,8,16,24,32,40,48,56,64,72,80,88,96,104,112,120,128,136,144,152,160..., dimensions={0} | all-to-all | bytes 65536 | tf_op jit(solution)/shard_map/all_to_all | solution.py:280
  40.3 0.0 copy-done
  40.3 0.0 copy-done.1
  40.3 1.0 %gradient.1.reflect_ref = f32[8,512]{1,0:T(8,128)S(1)} custom-call(s32[1,8]{1,0:T(1,128)} %bitcast.16, f32[64,128]{1,0:T(8,128)S(1)} %bitcast.12, f32[1,8,2,256]{3,2,1,0:T(2,128)S(1)} %copy-done.1, f32[8,1,64,512]{3,2,1,0:T(8,128)S(1)} %copy-done), custom_call_target="tpu_custom_call" | custom-call | tf_op jit(solution)/shard_map/gradient/pallas_call | solution.py:282
  41.3 13.1 %all-gather = f32[16,512]{1,0:T(8,128)S(1)} all-gather(f32[8,512]{1,0:T(8,128)S(1)} %gradient.1.reflect_ref), channel_id=2, replica_groups={{0,4},{1,5},{2,6},{3,7},{8,12},{9,13},{10,14},{11,15},{16,20},{17,21},{..., dimensions={0}, use_global_device_ids=true | all-gather | bytes 49152 | tf_op jit(solution)/shard_map/all_gather | solution.py:290
  54.4 1.8 %all-gather.1 = f32[16,512]{1,0:T(8,128)S(1)} all-gather(f32[8,512]{1,0:T(8,128)S(1)} %sum.1), channel_id=3, replica_groups={{0,8},{16,24},{32,40},{48,56},{64,72},{80,88},{96,104},{112,120},{128,1..., dimensions={0}, use_global_device_ids=true | all-gather | bytes 49152 | tf_op jit(solution)/shard_map/all_gather | solution.py:298
  56.3 15.1 %all_to_all.17.shares_ref = f32[8,2,8,512]{3,2,1,0:T(8,128)S(1)} all-to-all(f32[8,2,8,512]{3,2,1,0:T(8,128)S(1)} %copies.1), channel_id=1, replica_groups={{10,9,11,8,18,17,19,16},{14,13,15,12,22,21,23,20},{26,25,27,24,34,33,35..., dimensions={0} | all-to-all | bytes 524288 | tf_op jit(solution)/shard_map/all_to_all | solution.py:307
  71.3 1.2 %prior.1 = (f32[1,8,2,256]{3,2,1,0:T(2,128)}, f32[8,2,256]{2,1,0:T(2,128)}) custom-call(f32[8,2,8,512]{3,2,1,0:T(8,128)S(1)} %all_to_all.17.shares_ref, f32[1,8,2,256]{3,2,1,0:T(2,128)S(1)} %copy-done.1, f32[8,512]{1,0:T(8,128)S(1)} %gradient.1.reflect_ref), custom_call_target="tpu_custom_call" | custom-call | tf_op jit(solution)/shard_map/prior/pallas_call | solution.py:308
  (2 shorter events, 0.0 us)
Async XLA Ops:
  0.6 39.7 %copy-start = (f32[8,1,64,512]{3,2,1,0:T(8,128)S(1)}, f32[8,1,64,512]{3,2,1,0:T(8,128)}, u32[]{:S(2)}) copy-start(f32[8,1,64,512]{3,2,1,0:T(8,128)} %blocks_ref.3) | copy-start | bytes 3145732
  25.1 15.2 %copy-start.1 = (f32[1,8,2,256]{3,2,1,0:T(2,128)S(1)}, f32[1,8,2,256]{3,2,1,0:T(2,128)}, u32[]{:S(2)}) copy-start(f32[1,8,2,256]{3,2,1,0:T(2,128)} %states_ref.5) | copy-start | bytes 49156

commit v8 on v6

--- a/solution.py
+++ b/solution.py
@@ -10,6 +10,8 @@
 RELAX = 0.6
 BLOCK = 32
 LANES = 128
+FIRST_OF_HALF = (42, 22)
+MIDDLE_FIRST = (2, 1, 3, 0)
 
 SMEM = pl.BlockSpec(memory_space=pltpu.SMEM)
 VMEM = pl.BlockSpec(memory_space=pltpu.VMEM)
@@ -63,6 +65,7 @@
     projected = split_dot(states_ref[0, :, 0, :], blocks[:, :width], ((1,), (1,)))
     projected += split_dot(states_ref[0, :, 1, :], blocks[:, width:], ((1,), (1,)))
     step = pl.program_id(0)
+    tile = lax.axis_index("tile").astype(jnp.float32)
     per_vreg = LANES // foot
     blank = jnp.zeros((slices, LANES - share), jnp.float32)
     for local in range(views):
@@ -77,6 +80,7 @@
         first = band + jnp.concatenate([blank, measured_ref[local]], axis=1)
         second = jnp.concatenate([weights_ref[local], blank], axis=1)
         second = jnp.where(lane == share, base.astype(jnp.float32), second)
+        second = jnp.where(lane == share + 1, tile, second)
         start = view * 2 * slices
         out_ref[pl.ds(start, slices, stride=2), :] = first
         out_ref[pl.ds(start + 1, slices, stride=2), :] = second
@@ -94,6 +98,18 @@
     width = x.shape[1]
     all_three = lax.dot_general(onehot, thirds(x), (dims, ((), ())), preferred_element_type=jnp.float32)
     return all_three[:, :width] + (all_three[:, width : 2 * width] + all_three[:, 2 * width :])
+
+
+def group_orders(n_tile, n_agent):
+    half = n_agent // 2
+    groups = []
+    for agent in range(n_agent):
+        first = FIRST_OF_HALF[agent // half]
+        rest = [tile for tile in range(n_tile) if tile != first]
+        if agent >= half:
+            rest = rest[::-1]
+        groups.append([tile * n_agent + agent for tile in [first] + rest])
+    return groups
 
 
 def residual_kernel(in_ref, out_ref):
@@ -109,8 +125,11 @@
     for part in (1, 2):
         moved = pltpu.roll(placed, part, 0)
         total += pltpu.roll(moved, LANES - part * share, 1)
-    measured = pltpu.roll(first, share, 1)
-    residual = jnp.where(lane < share, second * (total - measured), 0.0)
+    tile = second[:, share + 1 : share + 2].astype(jnp.int32)
+    place = jnp.where(lane_iota((tiles, tiles)) == tile, 1.0, 0.0).astype(jnp.bfloat16)
+    ordered = select_dot(place, jnp.where(lane < share, second, first), ((0,), (0,)))
+    measured = pltpu.roll(ordered, share, 1)
+    residual = jnp.where(lane < share, ordered * (total - measured), 0.0)
     windows = residual
     for part in (1, 2):
         moved = pltpu.roll(residual, tiles - part, 0)
@@ -226,7 +245,7 @@
         for first in (0, half):
             second = first if odd // per_x == even // per_x else half - first
             groups.append(
-                [odd * n_agent + first + y for y in range(half)] + [even * n_agent + second + y for y in range(half)]
+                [odd * n_agent + first + y for y in MIDDLE_FIRST] + [even * n_agent + second + y for y in MIDDLE_FIRST]
             )
     return groups
 
@@ -255,7 +274,9 @@
         out_shape=near_shape(2 * n_tile, LANES),
         name="project",
     )(starts, states, footprints, measured, weights)
-    bands = lax.all_to_all(sent.reshape(n_tile, 2, LANES), "tile", 0, 0, tiled=True)
+    axes = ("tile", "agent")
+    orders = group_orders(n_tile, n_agent)
+    bands = lax.all_to_all(sent.reshape(n_tile, 2, LANES), axes, 0, 0, tiled=True, axis_index_groups=orders)
     back = pl.pallas_call(
         residual_kernel,
         in_specs=[VMEM],
@@ -263,7 +284,7 @@
         out_shape=near_shape(n_tile, LANES),
         name="residual",
     )(near(bands.reshape(2 * n_tile, LANES)))
-    windows = lax.all_to_all(back.reshape(n_tile, 1, LANES), "tile", 0, 0, tiled=True)
+    windows = lax.all_to_all(back.reshape(n_tile, 1, LANES), axes, 0, 0, tiled=True, axis_index_groups=orders)
     states_near = near(states)
     reflect = pl.pallas_call(
         gradient_kernel,
@@ -289,7 +310,6 @@
         out_shape=near_shape(n_agent, 2, slices, pixels),
         name="copies",
     )(near(chip))
-    axes = ("tile", "agent")
     shares = lax.all_to_all(copies, axes, 0, 0, tiled=True, axis_index_groups=facing_groups(n_tile, n_agent, 16))
     new_states, prior = pl.pallas_call(
         prior_kernel,

time: 79.7 us -> 70.9 us (0.89)
  the two profiles are of different devices: /device:TPU:1 before, /device:TPU:16 now
where the time goes in v8:
time: 70.9 us; the launch traced here: 70.6 us
  blocking collectives  65.3 us (92%)
  Pallas kernels  4.6 us (6%)
    all_to_all x1, blocking collectives, shards(): lax.all_to_all(sent.reshape(n_tile, 2, LANES), axes, 0, 0, tiled=True, ax...  21.1 us
    all_to_all x1, blocking collectives, shards(): lax.all_to_all(back.reshape(n_tile, 1, LANES), axes, 0, 0, tiled=True, ax...  15.2 us
    all_to_all x1, blocking collectives, shards(): lax.all_to_all(copies, axes, 0, 0, tiled=True, axis_index_groups=facing_g...  14.1 us
    all_gather x1, blocking collectives, shards(): lax.all_gather(reflect, 'agent', axis=0, axis_index_groups=[[y, half + y]...  13.1 us
    pallas_call x1, Pallas kernels, shards(): pl.pallas_call(project_kernel, grid=(2,), in_specs=[SMEM, pl.BlockSpec(st...  1.82 us
    all_gather x1, blocking collectives, shards(): lax.all_gather(summed, 'tile', axis=0, axis_index_groups=[[t, t + 1] for...  1.82 us

profile of v8, /device:TPU:16, one launch (start us, length us, event | category | flops | bytes accessed | tf_op | source)
XLA Modules:
  0.0 70.6 jit_solution(849164244147277469)
XLA Ops:
  0.6 0.0 copy-start
  0.6 1.8 %project.1 = f32[128,128]{1,0:T(8,128)S(1)} custom-call(s32[1,8]{1,0:T(1,128)} %bitcast.15, f32[1,8,2,256]{3,2,1,0:T(2,128)} %states_ref.5, f32[8,1,64,512]{3,2,1,0:T(8,128)} %blocks_ref.3, f32[8,8,32]{2,1,0:T(8,128)} %measured_ref.1, f32[8,8,32]{2,1,0:T(8,128)} %weights_ref.1), custom_call_target="tpu_custom_call" | custom-call | tf_op jit(solution)/shard_map/project/pallas_call | solution.py:263
  2.5 21.1 %all_to_all.15 = f32[64,2,128]{2,1,0:T(2,128)S(1)} all-to-all(f32[64,2,128]{2,1,0:T(2,128)S(1)} %bitcast.9), channel_id=1, replica_groups={{336,0,8,16,24,32,40,48,56,64,72,80,88,96,104,112,120,128,136,144,152,1..., dimensions={0} | all-to-all | bytes 131072 | tf_op jit(solution)/shard_map/all_to_all | solution.py:279
  23.6 0.6 residual.1
  24.2 0.0 copy-start.1
  24.2 15.2 %all_to_all.16 = f32[64,1,128]{2,1,0:T(1,128)S(1)} all-to-all(f32[64,1,128]{2,1,0:T(1,128)S(1)} %bitcast.11), channel_id=1, replica_groups={{336,0,8,16,24,32,40,48,56,64,72,80,88,96,104,112,120,128,136,144,152,1..., dimensions={0} | all-to-all | bytes 65536 | tf_op jit(solution)/shard_map/all_to_all | solution.py:287
  39.3 0.0 copy-done
  39.3 0.0 copy-done.1
  39.3 1.0 %gradient.1.reflect_ref = f32[8,512]{1,0:T(8,128)S(1)} custom-call(s32[1,8]{1,0:T(1,128)} %bitcast.16, f32[64,128]{1,0:T(8,128)S(1)} %bitcast.12, f32[1,8,2,256]{3,2,1,0:T(2,128)S(1)} %copy-done.1, f32[8,1,64,512]{3,2,1,0:T(8,128)S(1)} %copy-done), custom_call_target="tpu_custom_call" | custom-call | tf_op jit(solution)/shard_map/gradient/pallas_call | solution.py:289
  40.3 13.1 %all-gather = f32[16,512]{1,0:T(8,128)S(1)} all-gather(f32[8,512]{1,0:T(8,128)S(1)} %gradient.1.reflect_ref), channel_id=2, replica_groups={{0,4},{1,5},{2,6},{3,7},{8,12},{9,13},{10,14},{11,15},{16,20},{17,21},{..., dimensions={0}, use_global_device_ids=true | all-gather | bytes 49152 | tf_op jit(solution)/shard_map/all_gather | solution.py:297
  53.4 1.8 %all-gather.1 = f32[16,512]{1,0:T(8,128)S(1)} all-gather(f32[8,512]{1,0:T(8,128)S(1)} %sum.1), channel_id=3, replica_groups={{0,8},{16,24},{32,40},{48,56},{64,72},{80,88},{96,104},{112,120},{128,1..., dimensions={0}, use_global_device_ids=true | all-gather | bytes 49152 | tf_op jit(solution)/shard_map/all_gather | solution.py:305
  55.3 14.1 %all_to_all.17.shares_ref = f32[8,2,8,512]{3,2,1,0:T(8,128)S(1)} all-to-all(f32[8,2,8,512]{3,2,1,0:T(8,128)S(1)} %copies.1), channel_id=1, replica_groups={{10,9,11,8,18,17,19,16},{14,13,15,12,22,21,23,20},{26,25,27,24,34,33,35..., dimensions={0} | all-to-all | bytes 524288 | tf_op jit(solution)/shard_map/all_to_all | solution.py:313
  69.4 1.2 %prior.1 = (f32[1,8,2,256]{3,2,1,0:T(2,128)}, f32[8,2,256]{2,1,0:T(2,128)}) custom-call(f32[8,2,8,512]{3,2,1,0:T(8,128)S(1)} %all_to_all.17.shares_ref, f32[1,8,2,256]{3,2,1,0:T(2,128)S(1)} %copy-done.1, f32[8,512]{1,0:T(8,128)S(1)} %gradient.1.reflect_ref), custom_call_target="tpu_custom_call" | custom-call | tf_op jit(solution)/shard_map/prior/pallas_call | solution.py:314
  (2 shorter events, 0.0 us)
Async XLA Ops:
  0.6 38.7 %copy-start = (f32[8,1,64,512]{3,2,1,0:T(8,128)S(1)}, f32[8,1,64,512]{3,2,1,0:T(8,128)}, u32[]{:S(2)}) copy-start(f32[8,1,64,512]{3,2,1,0:T(8,128)} %blocks_ref.3) | copy-start | bytes 3145732
  24.2 15.2 %copy-start.1 = (f32[1,8,2,256]{3,2,1,0:T(2,128)S(1)}, f32[1,8,2,256]{3,2,1,0:T(2,128)}, u32[]{:S(2)}) copy-start(f32[1,8,2,256]{3,2,1,0:T(2,128)} %states_ref.5) | copy-start | bytes 49156

commit v9 on v8

--- a/solution.py
+++ b/solution.py
@@ -10,7 +10,7 @@
 RELAX = 0.6
 BLOCK = 32
 LANES = 128
-FIRST_OF_HALF = (42, 22)
+FIRST_OF_HALF = (43, 23)
 MIDDLE_FIRST = (2, 1, 3, 0)
 
 SMEM = pl.BlockSpec(memory_space=pltpu.SMEM)

time: 70.9 us -> 70.3 us (level)
  no operation moved by 1% of the time
where the time goes in v9:
time: 70.3 us; the launch traced here: 70 us
  blocking collectives  64.7 us (92%)
  Pallas kernels  4.6 us (7%)
    all_to_all x1, blocking collectives, shards(): lax.all_to_all(sent.reshape(n_tile, 2, LANES), axes, 0, 0, tiled=True, ax...  20.8 us
    all_to_all x1, blocking collectives, shards(): lax.all_to_all(back.reshape(n_tile, 1, LANES), axes, 0, 0, tiled=True, ax...  14.9 us
    all_to_all x1, blocking collectives, shards(): lax.all_to_all(copies, axes, 0, 0, tiled=True, axis_index_groups=facing_g...  14.1 us
    all_gather x1, blocking collectives, shards(): lax.all_gather(reflect, 'agent', axis=0, axis_index_groups=[[y, half + y]...  13.1 us
    pallas_call x1, Pallas kernels, shards(): pl.pallas_call(project_kernel, grid=(2,), in_specs=[SMEM, pl.BlockSpec(st...  1.82 us
    all_gather x1, blocking collectives, shards(): lax.all_gather(summed, 'tile', axis=0, axis_index_groups=[[t, t + 1] for...  1.82 us

profile of v9, /device:TPU:16, one launch (start us, length us, event | category | flops | bytes accessed | tf_op | source)
XLA Modules:
  0.0 70.0 jit_solution(11557429807306386465)
XLA Ops:
  0.6 0.0 copy-start
  0.6 1.8 %project.1 = f32[128,128]{1,0:T(8,128)S(1)} custom-call(s32[1,8]{1,0:T(1,128)} %bitcast.15, f32[1,8,2,256]{3,2,1,0:T(2,128)} %states_ref.5, f32[8,1,64,512]{3,2,1,0:T(8,128)} %blocks_ref.3, f32[8,8,32]{2,1,0:T(8,128)} %measured_ref.1, f32[8,8,32]{2,1,0:T(8,128)} %weights_ref.1), custom_call_target="tpu_custom_call" | custom-call | tf_op jit(solution)/shard_map/project/pallas_call | solution.py:263
  2.5 20.8 %all_to_all.15 = f32[64,2,128]{2,1,0:T(2,128)S(1)} all-to-all(f32[64,2,128]{2,1,0:T(2,128)S(1)} %bitcast.9), channel_id=1, replica_groups={{344,0,8,16,24,32,40,48,56,64,72,80,88,96,104,112,120,128,136,144,152,1..., dimensions={0} | all-to-all | bytes 131072 | tf_op jit(solution)/shard_map/all_to_all | solution.py:279
  23.3 0.6 residual.1
  23.9 0.0 copy-start.1
  23.9 14.9 %all_to_all.16 = f32[64,1,128]{2,1,0:T(1,128)S(1)} all-to-all(f32[64,1,128]{2,1,0:T(1,128)S(1)} %bitcast.11), channel_id=1, replica_groups={{344,0,8,16,24,32,40,48,56,64,72,80,88,96,104,112,120,128,136,144,152,1..., dimensions={0} | all-to-all | bytes 65536 | tf_op jit(solution)/shard_map/all_to_all | solution.py:287
  38.8 0.0 copy-done
  38.8 0.0 copy-done.1
  38.8 1.0 %gradient.1.reflect_ref = f32[8,512]{1,0:T(8,128)S(1)} custom-call(s32[1,8]{1,0:T(1,128)} %bitcast.16, f32[64,128]{1,0:T(8,128)S(1)} %bitcast.12, f32[1,8,2,256]{3,2,1,0:T(2,128)S(1)} %copy-done.1, f32[8,1,64,512]{3,2,1,0:T(8,128)S(1)} %copy-done), custom_call_target="tpu_custom_call" | custom-call | tf_op jit(solution)/shard_map/gradient/pallas_call | solution.py:289
  39.8 13.1 %all-gather = f32[16,512]{1,0:T(8,128)S(1)} all-gather(f32[8,512]{1,0:T(8,128)S(1)} %gradient.1.reflect_ref), channel_id=2, replica_groups={{0,4},{1,5},{2,6},{3,7},{8,12},{9,13},{10,14},{11,15},{16,20},{17,21},{..., dimensions={0}, use_global_device_ids=true | all-gather | bytes 49152 | tf_op jit(solution)/shard_map/all_gather | solution.py:297
  52.9 1.8 %all-gather.1 = f32[16,512]{1,0:T(8,128)S(1)} all-gather(f32[8,512]{1,0:T(8,128)S(1)} %sum.1), channel_id=3, replica_groups={{0,8},{16,24},{32,40},{48,56},{64,72},{80,88},{96,104},{112,120},{128,1..., dimensions={0}, use_global_device_ids=true | all-gather | bytes 49152 | tf_op jit(solution)/shard_map/all_gather | solution.py:305
  54.7 14.1 %all_to_all.17.shares_ref = f32[8,2,8,512]{3,2,1,0:T(8,128)S(1)} all-to-all(f32[8,2,8,512]{3,2,1,0:T(8,128)S(1)} %copies.1), channel_id=1, replica_groups={{10,9,11,8,18,17,19,16},{14,13,15,12,22,21,23,20},{26,25,27,24,34,33,35..., dimensions={0} | all-to-all | bytes 524288 | tf_op jit(solution)/shard_map/all_to_all | solution.py:313
  68.8 1.2 %prior.1 = (f32[1,8,2,256]{3,2,1,0:T(2,128)}, f32[8,2,256]{2,1,0:T(2,128)}) custom-call(f32[8,2,8,512]{3,2,1,0:T(8,128)S(1)} %all_to_all.17.shares_ref, f32[1,8,2,256]{3,2,1,0:T(2,128)S(1)} %copy-done.1, f32[8,512]{1,0:T(8,128)S(1)} %gradient.1.reflect_ref), custom_call_target="tpu_custom_call" | custom-call | tf_op jit(solution)/shard_map/prior/pallas_call | solution.py:314
  (2 shorter events, 0.0 us)
Async XLA Ops:
  0.6 38.1 %copy-start = (f32[8,1,64,512]{3,2,1,0:T(8,128)S(1)}, f32[8,1,64,512]{3,2,1,0:T(8,128)}, u32[]{:S(2)}) copy-start(f32[8,1,64,512]{3,2,1,0:T(8,128)} %blocks_ref.3) | copy-start | bytes 3145732
  23.9 14.9 %copy-start.1 = (f32[1,8,2,256]{3,2,1,0:T(2,128)S(1)}, f32[1,8,2,256]{3,2,1,0:T(2,128)}, u32[]{:S(2)}) copy-start(f32[1,8,2,256]{3,2,1,0:T(2,128)} %states_ref.5) | copy-start | bytes 49156
